TPU v7x, 256 devices: a whole 4x4x8 slice. The times are simulated.
256 devices in a mesh: gx: 32 (over z, x), gy: 4 (over y_lo, core), gz: 2 (over y_hi).
Axes of the slice: x: 4, y: 4 (y_hi: 2, y_lo: 2; y = y_hi * 2 + y_lo), z: 8, core: 2. Of those that a mesh axis runs over, the one named last changes fastest.
Arguments:
- coarse_fields: float32 [4, 512, 64, 256], P(None, 'gx', 'gy', 'gz'), may hold values from -6 to 6
- coarse_wind: float32 [3, 512, 64, 256], P(None, 'gx', 'gy', 'gz'), may hold values from -0.4 to 0.4
- fine_fields: float32 [4, 1024, 64, 256], P(None, 'gx', 'gy', 'gz'), may hold values from -6 to 6
- fine_wind: float32 [3, 1024, 64, 256], P(None, 'gx', 'gy', 'gz'), may hold values from -0.4 to 0.4
- fine_owner: int32 [32, 4, 2], P('gx', 'gy', 'gz'), may hold values from 0 to 31, as said below
Outputs:
- coarse_next: float32 [4, 512, 64, 256], P(None, 'gx', 'gy', 'gz')
- fine_next: float32 [4, 1024, 64, 256], P(None, 'gx', 'gy', 'gz')
Inputs may be any that keep to these rules, and one draw needn't show every extreme that they name: `fine_owner`: in each row of fine boxes along the first direction (fixed second and third index), fine box i refines coarse box (i + r) mod 32 for an offset r of that row, so every row names every coarse box once.
All inputs are finite; a program needn't handle non-finite values.
Results may differ from a plain program's by a relative error of at most 0.0003.
Values sent between devices are 32-bit elements; how exact they have to be, the bound alone decides.
A program may use at most 128 MiB of HBM per device.

v0:
```python
import math

import jax
import jax.numpy as jnp
from jax import lax
from jax.sharding import PartitionSpec as P

diffusion = 0.05
section_weights = (1.0 / 3.0, 0.5, 1.0)


def extended(array, sides, width, wrap):
    for axis, dim in sides:
        size, length = (lax.axis_size(axis), array.shape[dim])
        up = [(i, (i + 1) % size) for i in range(size if wrap else size - 1)]
        down = [(j, i) for i, j in up]
        last = lax.slice_in_dim(array, length - width, length, axis=dim)
        first = lax.slice_in_dim(array, 0, width, axis=dim)
        before = lax.ppermute(last, axis, up)
        after = lax.ppermute(first, axis, down)
        array = jnp.concatenate([before, array, after], axis=dim)
    return array


def tendency(padded, velocity):
    center = padded[:, 1:-1, 1:-1, 1:-1]
    along_first = padded[:, 2:, 1:-1, 1:-1] - padded[:, :-2, 1:-1, 1:-1]
    along_second = padded[:, 1:-1, 2:, 1:-1] - padded[:, 1:-1, :-2, 1:-1]
    along_third = padded[:, 1:-1, 1:-1, 2:] - padded[:, 1:-1, 1:-1, :-2]
    beside_all = (
        padded[:, 2:, 1:-1, 1:-1]
        + padded[:, :-2, 1:-1, 1:-1]
        + (padded[:, 1:-1, 2:, 1:-1] + padded[:, 1:-1, :-2, 1:-1])
        + (padded[:, 1:-1, 1:-1, 2:] + padded[:, 1:-1, 1:-1, :-2])
    )
    advect = velocity[0] * along_first + velocity[1] * along_second + velocity[2] * along_third
    return -0.5 * advect + diffusion * (beside_all - 6.0 * center)


def refine(coarse, direction):
    length = coarse.shape[direction]
    low_part = lax.slice_in_dim(coarse, 0, length - 1, axis=direction)
    high_part = lax.slice_in_dim(coarse, 1, length, axis=direction)
    odd_cells = 0.75 * low_part + 0.25 * high_part
    even_cells = 0.25 * low_part + 0.75 * high_part
    paired = jnp.stack((odd_cells, even_cells), axis=direction + 1)
    target = list(coarse.shape)
    target[direction] = 2 * (length - 1)
    return paired.reshape(target)


def coarse_slabs(padded, lead_y, span_y, lead_z, span_z):
    rows_y = jnp.concatenate(
        (padded[:, :, lead_y : lead_y + 2], padded[:, :, lead_y + span_y : lead_y + span_y + 2]),
        axis=2,
    )
    slab_y = rows_y[:, :, :, lead_z : lead_z + span_z + 2]
    rows_z = jnp.concatenate(
        (
            padded[:, :, :, lead_z : lead_z + 2],
            padded[:, :, :, lead_z + span_z : lead_z + span_z + 2],
        ),
        axis=3,
    )
    slab_z = rows_z[:, :, lead_y : lead_y + span_y + 2, :]
    return (slab_y, slab_z)


def slab_faces(slab_y, slab_z):
    wide_y = refine(slab_y, 1)[:, 1:-1]
    low_y = 0.75 * wide_y[:, :, 0] + 0.25 * wide_y[:, :, 1]
    high_y = 0.25 * wide_y[:, :, 2] + 0.75 * wide_y[:, :, 3]
    faces_y = refine(jnp.stack((low_y, high_y), axis=2), 3)[:, :, :, 1:-1]
    wide_z = refine(refine(slab_z, 1)[:, 1:-1], 2)[:, :, 1:-1]
    low_z = 0.75 * wide_z[:, :, :, 0] + 0.25 * wide_z[:, :, :, 1]
    high_z = 0.25 * wide_z[:, :, :, 2] + 0.75 * wide_z[:, :, :, 3]
    faces_z = jnp.stack((low_z, high_z), axis=3)
    return (faces_y, faces_z)


def fine_padded(widened, faces_y, faces_z):
    inner = widened[:, 1:-1]
    middle = jnp.concatenate((faces_z[:, :, :, 0:1], inner, faces_z[:, :, :, 1:2]), axis=3)
    side_low = jnp.pad(faces_y[:, :, 0:1], ((0, 0), (0, 0), (0, 0), (1, 1)))
    side_high = jnp.pad(faces_y[:, :, 1:2], ((0, 0), (0, 0), (0, 0), (1, 1)))
    middle = jnp.concatenate((side_low, middle, side_high), axis=2)
    end_low = jnp.pad(widened[:, 0:1], ((0, 0), (0, 0), (1, 1), (1, 1)))
    end_high = jnp.pad(widened[:, -1:], ((0, 0), (0, 0), (1, 1), (1, 1)))
    return jnp.concatenate((end_low, middle, end_high), axis=1)


def coarsen(fine):
    blocks = fine.reshape(
        fine.shape[0], fine.shape[1] // 2, 2, fine.shape[2] // 2, 2, fine.shape[3] // 2, 2
    )
    return 0.125 * jnp.sum(blocks, axis=(2, 4, 6))


def pack_parts(payload):
    return jnp.concatenate([member.reshape(member.shape[0], -1) for member in payload], axis=1)


def unpack_parts(packed, shapes):
    pieces = []
    cursor = 0
    for target in shapes:
        extent = math.prod(target[1:])
        pieces.append(packed[:, cursor : cursor + extent].reshape(target))
        cursor += extent
    return tuple(pieces)


def send_forward(payload, cycle_size, offset, position):
    shapes = [member.shape for member in payload]
    packed = pack_parts(payload)
    gathered = lax.all_gather(packed[None], "gx", axis=0, tiled=True)
    arrived = lax.dynamic_index_in_dim(
        gathered, (position + offset) % cycle_size, 0, keepdims=False
    )
    return unpack_parts(arrived, shapes)


def send_back(averaged, cycle_size, offset, position):
    packed = averaged.reshape(averaged.shape[0], -1)
    gathered = lax.all_gather(packed[None], "gx", axis=0, tiled=True)
    arrived = lax.dynamic_index_in_dim(
        gathered, (position - offset) % cycle_size, 0, keepdims=False
    )
    return arrived.reshape(averaged.shape)


def shards(coarse_fields, coarse_wind, fine_fields, fine_wind, fine_owner):
    cycle_size = lax.axis_size("gx")
    position = lax.axis_index("gx")
    offset = (fine_owner[0, 0, 0] - position) % cycle_size
    lead_y = coarse_fields.shape[2] // 4
    span_y = coarse_fields.shape[2] // 2
    lead_z = coarse_fields.shape[3] // 4
    span_z = coarse_fields.shape[3] // 2
    coarse_state = coarse_fields
    fine_state = fine_fields
    for fraction in section_weights:
        sides = extended(coarse_state, (("gx", 1), ("gy", 2)), 1, True)
        padded = extended(sides, (("gz", 3),), 1, False)
        coarse_rate = tendency(padded, coarse_wind)
        slab_y, slab_z = coarse_slabs(padded, lead_y, span_y, lead_z, span_z)
        faces_y, faces_z = slab_faces(slab_y, slab_z)
        faces_y, faces_z = send_forward((faces_y, faces_z), cycle_size, offset, position)
        widened = extended(fine_state, (("gx", 1),), 1, True)
        fine_rate = tendency(fine_padded(widened, faces_y, faces_z), fine_wind)
        coarse_state = coarse_fields + fraction * coarse_rate
        fine_state = fine_fields + fraction * fine_rate
    averaged = send_back(coarsen(fine_state), cycle_size, offset, position)
    column = jnp.concatenate(
        (
            coarse_state[:, :, lead_y : lead_y + span_y, :lead_z],
            averaged,
            coarse_state[:, :, lead_y : lead_y + span_y, lead_z + span_z :],
        ),
        axis=3,
    )
    coarse_next = jnp.concatenate(
        (coarse_state[:, :, :lead_y], column, coarse_state[:, :, lead_y + span_y :]), axis=2
    )
    return (coarse_next, fine_state)


def solution(mesh):
    return jax.shard_map(
        shards,
        mesh=mesh,
        in_specs=(
            P(None, "gx", "gy", "gz"),
            P(None, "gx", "gy", "gz"),
            P(None, "gx", "gy", "gz"),
            P(None, "gx", "gy", "gz"),
            P("gx", "gy", "gz"),
        ),
        out_specs=(P(None, "gx", "gy", "gz"), P(None, "gx", "gy", "gz")),
        check_vma=False,
    )
```

profile of v0, /device:TPU:24, one launch (start us, length us, event | category | flops | bytes accessed | tf_op | source)
XLA Modules:
  0.0 454.7 jit_solution(6036083444465853417)
XLA Ops:
  9.5 6.6 %collective-permute-start = (f32[4,1,16,128]{3,2,1,0:T(8,128)S(1)}, f32[4,1,16,128]{3,2,1,0:T(8,128)S(1)}, u32[]{:S(2)}, u32[]{:S(2)}) collective-permute-start(f32[4,1,16,128]{3,2,1,0:T(8,128)S(1)} %get-tuple-element.55), channel_id=1, source_target_pairs={{8,0},{16,8},{24,16},{32,24},{40,32},{48,40},{56,48},{64,56},{72,6... | collective-permute-start | bytes 98312 | tf_op jit(solution)/shard_map/ppermute | solution.py:20
  28.3 3.1 collective-permute-start.4
  36.4 2.4 collective-permute-done.5
  45.5 2.9 multiply_add_fusion.3
  48.4 5.3 %collective-permute-start.6 = (f32[4,1,16,128]{3,2,1,0:T(8,128)S(1)}, f32[4,1,16,128]{3,2,1,0:T(8,128)S(1)}, u32[]{:S(2)}, u32[]{:S(2)}) collective-permute-start(f32[4,1,16,128]{3,2,1,0:T(8,128)S(1)} %get-tuple-element.54), channel_id=1, source_target_pairs={{8,0},{16,8},{24,16},{32,24},{40,32},{48,40},{56,48},{64,56},{72,6... | collective-permute-start | bytes 98312 | tf_op jit(solution)/shard_map/ppermute | solution.py:20
  61.0 2.3 copy.604
  63.3 2.3 copy.602
  65.6 4.3 collective-permute-start.10
  91.3 5.5 %collective-permute-start.12 = (f32[4,1,16,128]{3,2,1,0:T(8,128)S(1)}, f32[4,1,16,128]{3,2,1,0:T(8,128)S(1)}, u32[]{:S(2)}, u32[]{:S(2)}) collective-permute-start(f32[4,1,16,128]{3,2,1,0:T(8,128)S(1)} %get-tuple-element.52), channel_id=1, source_target_pairs={{8,0},{16,8},{24,16},{32,24},{40,32},{48,40},{56,48},{64,56},{72,6... | collective-permute-start | bytes 98312 | tf_op jit(solution)/shard_map/ppermute | solution.py:20
  96.8 2.3 collective-permute-done.13
  104.1 2.3 copy.614
  107.5 6.4 %collective-permute-start.16 = (f32[4,18,18,1]{2,0,3,1:T(4,128)}, f32[4,18,18,1]{2,0,3,1:T(4,128)S(1)}, u32[]{:S(2)}, u32[]{:S(2)}) collective-permute-start(f32[4,18,18,1]{2,0,3,1:T(4,128)} %copy.612), channel_id=1, source_target_pairs={{1,0},{3,2},{5,4},{7,6},{9,8},{11,10},{13,12},{15,14},{17,16},{19,... | collective-permute-start | bytes 15560 | tf_op jit(solution)/shard_map/ppermute | solution.py:20
  129.7 5.4 %collective-permute-start.18 = (f32[4,1,16,128]{3,2,1,0:T(8,128)}, f32[4,1,16,128]{3,2,1,0:T(8,128)}, u32[]{:S(2)}, u32[]{:S(2)}) collective-permute-start(f32[4,1,16,128]{3,2,1,0:T(8,128)} %get-tuple-element.19), channel_id=1, source_target_pairs={{8,0},{16,8},{24,16},{32,24},{40,32},{48,40},{56,48},{64,56},{72,6... | collective-permute-start | bytes 98312 | tf_op jit(solution)/shard_map/ppermute | solution.py:20
  137.8 70.3 %all-gather.15.cloned.1.call-done = f32[32,4,9216]{2,1,0:T(4,128)} async-done(((f32[1,4,9216]{2,1,0:T(4,128)}), f32[32,4,9216]{2,1,0:T(4,128)}) %all-gather.15.cloned.1.call-update) | async-done | bytes 4718608 | tf_op jit(solution)/shard_map/all_gather | solution.py:116
  214.0 4.7 %copy.664 = f32[4,32,16,1]{3,2,1,0:T(8,128)S(1)} copy(f32[4,32,16,1]{0,3,2,1:T(1,128)} %get-tuple-element.49) | data formatting | bytes 16384 | tf_op jit(solution)/shard_map/slice | solution.py:83
  218.7 5.6 %copy.665 = f32[4,32,16,1]{3,2,1,0:T(8,128)} copy(f32[4,32,16,1]{0,3,2,1:T(1,128)} %get-tuple-element.50) | data formatting | bytes 16384 | tf_op jit(solution)/shard_map/slice | solution.py:83
  224.3 4.7 %multiply_add_fusion.1 = f32[4,32,16,128]{3,2,1,0:T(8,128)S(1)} fusion(f32[4,32,16,128]{3,2,1,0:T(8,128)S(1)} %copy-done, f32[4,32,16,1]{3,2,1,0:T(8,128)} %copy.665, f32[4,32,16,1]{3,2,1,0:T(8,128)S(1)} %copy.664, f32[4,32,1,130]{3,2,1,0:T(1,128)} %pad.41, f32[4,32,1,130]{3,2,1,0:T(1,128)} %pad.40, f32[4,1,16,128]{3,2,1,0:T(8,128)} %collective-permute-done.18, ...), kind=kLoop, calls=%fused_computation.68 | loop fusion | flops 11534336 | bytes 3098624 | tf_op jit(solution)/shard_map/add | solution.py:152
  230.3 5.3 %collective-permute-start.20 = (f32[4,1,16,128]{3,2,1,0:T(8,128)S(1)}, f32[4,1,16,128]{3,2,1,0:T(8,128)}, u32[]{:S(2)}, u32[]{:S(2)}) collective-permute-start(f32[4,1,16,128]{3,2,1,0:T(8,128)S(1)} %get-tuple-element.17), channel_id=1, source_target_pairs={{8,0},{16,8},{24,16},{32,24},{40,32},{48,40},{56,48},{64,56},{72,6... | collective-permute-start | bytes 98312 | tf_op jit(solution)/shard_map/ppermute | solution.py:20
  237.4 4.7 %copy.668 = f32[4,32,16,1]{3,2,1,0:T(8,128)} copy(f32[4,32,16,1]{0,3,2,1:T(1,128)S(1)} %get-tuple-element.47) | data formatting | bytes 16384 | tf_op jit(solution)/shard_map/slice | solution.py:83
  242.0 4.7 %copy.669 = f32[4,32,16,1]{3,2,1,0:T(8,128)} copy(f32[4,32,16,1]{0,3,2,1:T(1,128)S(1)} %get-tuple-element.48) | data formatting | bytes 16384 | tf_op jit(solution)/shard_map/slice | solution.py:83
  247.3 7.4 %multiply_add_fusion = f32[4,32,16,128]{3,2,1,0:T(8,128)S(1)} fusion(f32[4,32,16,128]{3,2,1,0:T(8,128)S(1)} %copy-done, f32[4,32,16,128]{3,2,1,0:T(8,128)} %copy-done.2, f32[4,32,16,1]{3,2,1,0:T(8,128)} %copy.669, f32[4,32,16,1]{3,2,1,0:T(8,128)} %copy.668, f32[4,32,1,130]{3,2,1,0:T(1,128)} %pad.44, f32[4,32,1,130]{3,2,1,0:T(1,128)S(1)} %pad.39, ...), kind=kLoop, calls=%fused_computation.67 | loop fusion | flops 11534336 | bytes 4147200 | tf_op jit(solution)/shard_map/add | solution.py:152
  255.4 5.5 %collective-permute-start.22 = (f32[4,1,16,128]{3,2,1,0:T(8,128)}, f32[4,1,16,128]{3,2,1,0:T(8,128)}, u32[]{:S(2)}, u32[]{:S(2)}) collective-permute-start(f32[4,1,16,128]{3,2,1,0:T(8,128)} %get-tuple-element.15), channel_id=1, source_target_pairs={{8,0},{16,8},{24,16},{32,24},{40,32},{48,40},{56,48},{64,56},{72,6... | collective-permute-start | bytes 98312 | tf_op jit(solution)/shard_map/ppermute | solution.py:20
  260.9 29.9 %all-gather.13.cloned.1.call-done = f32[32,4,9216]{2,1,0:T(4,128)} async-done(((f32[1,4,9216]{2,1,0:T(4,128)}), f32[32,4,9216]{2,1,0:T(4,128)}) %all-gather.13.cloned.1.call-update) | async-done | bytes 4718608 | tf_op jit(solution)/shard_map/all_gather | solution.py:116
  294.5 2.6 fusion.33
  298.6 5.6 %copy.672 = f32[4,32,16,1]{3,2,1,0:T(8,128)} copy(f32[4,32,16,1]{0,3,2,1:T(1,128)} %get-tuple-element.45) | data formatting | bytes 16384 | tf_op jit(solution)/shard_map/slice | solution.py:83
  304.2 5.6 %copy.673 = f32[4,32,16,1]{3,2,1,0:T(8,128)} copy(f32[4,32,16,1]{0,3,2,1:T(1,128)} %get-tuple-element.46) | data formatting | bytes 16384 | tf_op jit(solution)/shard_map/slice | solution.py:83
  309.8 6.6 %add_add_fusion = f32[4,32,16,128]{3,2,1,0:T(8,128)} fusion(f32[4,32,16,128]{3,2,1,0:T(8,128)S(1)} %copy-done, f32[4,32,16,128]{3,2,1,0:T(8,128)S(1)} %multiply_add_fusion, f32[4,32,16,1]{3,2,1,0:T(8,128)} %copy.673, f32[4,32,16,1]{3,2,1,0:T(8,128)} %copy.672, f32[4,32,1,130]{3,2,1,0:T(1,128)} %pad.47, f32[4,32,1,130]{3,2,1,0:T(1,128)S(1)} %pad.38, ...), kind=kLoop, calls=%fused_computation.66 | loop fusion | flops 11272192 | bytes 4147200 | tf_op jit(solution)/shard_map/add | solution.py:152
  316.4 17.4 %copy.676 = f32[4,32,16,128]{0,3,2,1:T(8,128)} copy(f32[4,32,16,128]{3,2,1,0:T(8,128)} %add_add_fusion) | data formatting | bytes 2097152 | tf_op jit(solution)/shard_map/add | solution.py:152
  333.8 24.2 %reduce_sum.9 = f32[4,16,8,64]{0,3,2,1:T(8,128)} reduce(f32[4,16,2,8,2,64,2]{0,6,5,4,3,2,1:T(2,128)} %bitcast.106, f32[]{:T(128)} %constant.76.clone.1), dimensions={2,4,6}, to_apply=%region_0.1 | reduce | flops 229376 | bytes 1179652 | tf_op jit(solution)/shard_map/reduce_sum | solution.py:96
  358.0 5.0 %broadcast_multiply_fusion = f32[4,16,8,64]{0,3,2,1:T(8,128)} fusion(f32[4,16,8,64]{0,3,2,1:T(8,128)} %reduce_sum.9), kind=kLoop, calls=%fused_computation | loop fusion | flops 32768 | bytes 262144 | tf_op jit(solution)/shard_map/mul | solution.py:96
  363.0 3.6 copy.677
  369.6 76.1 %all-gather.11.cloned.1.call-done = f32[32,4,8192]{2,1,0:T(4,128)} async-done(((f32[1,4,8192]{2,1,0:T(4,128)}), f32[32,4,8192]{2,1,0:T(4,128)}) %all-gather.11.cloned.1.call-update) | async-done | bytes 4194320 | tf_op jit(solution)/shard_map/all_gather | solution.py:125
  (264 shorter events, 98.3 us)
Async XLA Ops:
  7.2 130.6 %all-gather.17.cloned.1.call-start = ((), (), s32[]{:S(2)}) async-start(), calls=%async_computation.3 | async-start | bytes 4866048 | tf_op jit(solution)/shard_map/all_gather | solution.py:116
  8.0 9.9 %collective-permute-start.1 = (f32[4,1,16,128]{3,2,1,0:T(8,128)S(1)}, f32[4,1,16,128]{3,2,1,0:T(8,128)S(1)}, u32[]{:S(2)}, u32[]{:S(2)}) collective-permute-start(f32[4,1,16,128]{3,2,1,0:T(8,128)S(1)} %get-tuple-element.56), channel_id=1, source_target_pairs={{0,8},{8,16},{16,24},{24,32},{32,40},{40,48},{48,56},{56,64},{64,7... | collective-permute-start | bytes 98312 | tf_op jit(solution)/shard_map/ppermute | solution.py:19
  9.5 9.5 %collective-permute-start = (f32[4,1,16,128]{3,2,1,0:T(8,128)S(1)}, f32[4,1,16,128]{3,2,1,0:T(8,128)S(1)}, u32[]{:S(2)}, u32[]{:S(2)}) collective-permute-start(f32[4,1,16,128]{3,2,1,0:T(8,128)S(1)} %get-tuple-element.55), channel_id=1, source_target_pairs={{8,0},{16,8},{24,16},{32,24},{40,32},{48,40},{56,48},{64,56},{72,6... | collective-permute-start | bytes 98312 | tf_op jit(solution)/shard_map/ppermute | solution.py:20
  19.1 1.7 collective-permute-start.2
  19.3 3.5 collective-permute-start.3
  28.3 11.0 %collective-permute-start.4 = (f32[4,18,18,1]{2,0,3,1:T(4,128)S(1)}, f32[4,18,18,1]{2,0,3,1:T(4,128)S(1)}, u32[]{:S(2)}, u32[]{:S(2)}) collective-permute-start(f32[4,18,18,1]{2,0,3,1:T(4,128)S(1)} %copy.592), channel_id=1, source_target_pairs={{1,0},{3,2},{5,4},{7,6},{9,8},{11,10},{13,12},{15,14},{17,16},{19,... | collective-permute-start | bytes 15560 | tf_op jit(solution)/shard_map/ppermute | solution.py:20
  31.4 7.4 %collective-permute-start.5 = (f32[4,18,18,1]{2,0,3,1:T(4,128)S(1)}, f32[4,18,18,1]{2,0,3,1:T(4,128)S(1)}, u32[]{:S(2)}, u32[]{:S(2)}) collective-permute-start(f32[4,18,18,1]{2,0,3,1:T(4,128)S(1)} %copy.594), channel_id=1, source_target_pairs={{0,1},{2,3},{4,5},{6,7},{8,9},{10,11},{12,13},{14,15},{16,17},{18,... | collective-permute-start | bytes 15560 | tf_op jit(solution)/shard_map/ppermute | solution.py:19
  43.2 164.9 %all-gather.15.cloned.1.call-start = ((), (), s32[]{:S(2)}) async-start(), calls=%async_computation.2 | async-start | bytes 4866048 | tf_op jit(solution)/shard_map/all_gather | solution.py:116
  43.4 45.8 %copy-start.5 = (f32[16,16,128]{2,1,0:T(8,128)}, f32[16,16,128]{2,1,0:T(8,128)S(1)}, u32[]{:S(2)}) copy-start(f32[16,16,128]{2,1,0:T(8,128)S(1)} %get-tuple-element.57) | copy-start | bytes 393220
  43.4 45.7 %copy-start.7 = (f32[16,16,128]{2,1,0:T(8,128)}, f32[16,16,128]{2,1,0:T(8,128)S(1)}, u32[]{:S(2)}) copy-start(f32[16,16,128]{2,1,0:T(8,128)S(1)} %get-tuple-element.58) | copy-start | bytes 393220
  43.4 45.7 %copy-start.9 = (f32[16,16,128]{2,1,0:T(8,128)}, f32[16,16,128]{2,1,0:T(8,128)S(1)}, u32[]{:S(2)}) copy-start(f32[16,16,128]{2,1,0:T(8,128)S(1)} %get-tuple-element.59) | copy-start | bytes 393220
  48.4 7.3 %collective-permute-start.7 = (f32[4,1,16,128]{3,2,1,0:T(8,128)S(1)}, f32[4,1,16,128]{3,2,1,0:T(8,128)S(1)}, u32[]{:S(2)}, u32[]{:S(2)}) collective-permute-start(f32[4,1,16,128]{3,2,1,0:T(8,128)S(1)} %get-tuple-element.53), channel_id=1, source_target_pairs={{0,8},{8,16},{16,24},{24,32},{32,40},{40,48},{48,56},{56,64},{64,7... | collective-permute-start | bytes 98312 | tf_op jit(solution)/shard_map/ppermute | solution.py:19
  48.4 7.2 %collective-permute-start.6 = (f32[4,1,16,128]{3,2,1,0:T(8,128)S(1)}, f32[4,1,16,128]{3,2,1,0:T(8,128)S(1)}, u32[]{:S(2)}, u32[]{:S(2)}) collective-permute-start(f32[4,1,16,128]{3,2,1,0:T(8,128)S(1)} %get-tuple-element.54), channel_id=1, source_target_pairs={{8,0},{16,8},{24,16},{32,24},{40,32},{48,40},{56,48},{64,56},{72,6... | collective-permute-start | bytes 98312 | tf_op jit(solution)/shard_map/ppermute | solution.py:20
  55.7 1.9 collective-permute-start.8
  55.9 3.5 collective-permute-start.9
  65.6 14.3 %collective-permute-start.10 = (f32[4,18,18,1]{2,0,3,1:T(4,128)}, f32[4,18,18,1]{2,0,3,1:T(4,128)}, u32[]{:S(2)}, u32[]{:S(2)}) collective-permute-start(f32[4,18,18,1]{2,0,3,1:T(4,128)} %copy.602), channel_id=1, source_target_pairs={{1,0},{3,2},{5,4},{7,6},{9,8},{11,10},{13,12},{15,14},{17,16},{19,... | collective-permute-start | bytes 15560 | tf_op jit(solution)/shard_map/ppermute | solution.py:20
  69.9 8.7 %collective-permute-start.11 = (f32[4,18,18,1]{2,0,3,1:T(4,128)}, f32[4,18,18,1]{2,0,3,1:T(4,128)}, u32[]{:S(2)}, u32[]{:S(2)}) collective-permute-start(f32[4,18,18,1]{2,0,3,1:T(4,128)} %copy.604), channel_id=1, source_target_pairs={{0,1},{2,3},{4,5},{6,7},{8,9},{10,11},{12,13},{14,15},{16,17},{18,... | collective-permute-start | bytes 15560 | tf_op jit(solution)/shard_map/ppermute | solution.py:19
  85.4 205.5 %all-gather.13.cloned.1.call-start = ((), (), s32[]{:S(2)}) async-start(), calls=%async_computation.1 | async-start | bytes 4866048 | tf_op jit(solution)/shard_map/all_gather | solution.py:116
  91.2 7.9 %collective-permute-start.13 = (f32[4,1,16,128]{3,2,1,0:T(8,128)S(1)}, f32[4,1,16,128]{3,2,1,0:T(8,128)S(1)}, u32[]{:S(2)}, u32[]{:S(2)}) collective-permute-start(f32[4,1,16,128]{3,2,1,0:T(8,128)S(1)} %get-tuple-element.51), channel_id=1, source_target_pairs={{0,8},{8,16},{16,24},{24,32},{32,40},{40,48},{48,56},{56,64},{64,7... | collective-permute-start | bytes 98312 | tf_op jit(solution)/shard_map/ppermute | solution.py:19
  91.3 7.8 %collective-permute-start.12 = (f32[4,1,16,128]{3,2,1,0:T(8,128)S(1)}, f32[4,1,16,128]{3,2,1,0:T(8,128)S(1)}, u32[]{:S(2)}, u32[]{:S(2)}) collective-permute-start(f32[4,1,16,128]{3,2,1,0:T(8,128)S(1)} %get-tuple-element.52), channel_id=1, source_target_pairs={{8,0},{16,8},{24,16},{32,24},{40,32},{48,40},{56,48},{64,56},{72,6... | collective-permute-start | bytes 98312 | tf_op jit(solution)/shard_map/ppermute | solution.py:20
  99.1 16.7 %copy-start.20 = (f32[4,1,16,128]{3,2,1,0:T(8,128)}, f32[4,1,16,128]{3,2,1,0:T(8,128)S(1)}, u32[]{:S(2)}) copy-start(f32[4,1,16,128]{3,2,1,0:T(8,128)S(1)} %collective-permute-done.12) | copy-start | bytes 98308
  99.1 1.9 collective-permute-start.14
  99.3 3.5 collective-permute-start.15
  107.5 15.4 %collective-permute-start.16 = (f32[4,18,18,1]{2,0,3,1:T(4,128)}, f32[4,18,18,1]{2,0,3,1:T(4,128)S(1)}, u32[]{:S(2)}, u32[]{:S(2)}) collective-permute-start(f32[4,18,18,1]{2,0,3,1:T(4,128)} %copy.612), channel_id=1, source_target_pairs={{1,0},{3,2},{5,4},{7,6},{9,8},{11,10},{13,12},{15,14},{17,16},{19,... | collective-permute-start | bytes 15560 | tf_op jit(solution)/shard_map/ppermute | solution.py:20
  114.0 7.7 %collective-permute-start.17 = (f32[4,18,18,1]{2,0,3,1:T(4,128)}, f32[4,18,18,1]{2,0,3,1:T(4,128)}, u32[]{:S(2)}, u32[]{:S(2)}) collective-permute-start(f32[4,18,18,1]{2,0,3,1:T(4,128)} %copy.614), channel_id=1, source_target_pairs={{0,1},{2,3},{4,5},{6,7},{8,9},{10,11},{12,13},{14,15},{16,17},{18,... | collective-permute-start | bytes 15560 | tf_op jit(solution)/shard_map/ppermute | solution.py:19
  128.6 317.1 %all-gather.11.cloned.1.call-start = ((), (), s32[]{:S(2)}) async-start(), calls=%async_computation | async-start | bytes 4325376 | tf_op jit(solution)/shard_map/all_gather | solution.py:125
  129.3 95.1 %collective-permute-start.19 = (f32[4,1,16,128]{3,2,1,0:T(8,128)}, f32[4,1,16,128]{3,2,1,0:T(8,128)}, u32[]{:S(2)}, u32[]{:S(2)}) collective-permute-start(f32[4,1,16,128]{3,2,1,0:T(8,128)} %get-tuple-element.18), channel_id=1, source_target_pairs={{0,8},{8,16},{16,24},{24,32},{32,40},{40,48},{48,56},{56,64},{64,7... | collective-permute-start | bytes 98312 | tf_op jit(solution)/shard_map/ppermute | solution.py:19
  129.7 94.7 %collective-permute-start.18 = (f32[4,1,16,128]{3,2,1,0:T(8,128)}, f32[4,1,16,128]{3,2,1,0:T(8,128)}, u32[]{:S(2)}, u32[]{:S(2)}) collective-permute-start(f32[4,1,16,128]{3,2,1,0:T(8,128)} %get-tuple-element.19), channel_id=1, source_target_pairs={{8,0},{16,8},{24,16},{32,24},{40,32},{48,40},{56,48},{64,56},{72,6... | collective-permute-start | bytes 98312 | tf_op jit(solution)/shard_map/ppermute | solution.py:20
  230.0 16.7 %collective-permute-start.21 = (f32[4,1,16,128]{3,2,1,0:T(8,128)S(1)}, f32[4,1,16,128]{3,2,1,0:T(8,128)S(1)}, u32[]{:S(2)}, u32[]{:S(2)}) collective-permute-start(f32[4,1,16,128]{3,2,1,0:T(8,128)S(1)} %get-tuple-element.16), channel_id=1, source_target_pairs={{0,8},{8,16},{16,24},{24,32},{32,40},{40,48},{48,56},{56,64},{64,7... | collective-permute-start | bytes 98312 | tf_op jit(solution)/shard_map/ppermute | solution.py:19
  230.3 17.0 %collective-permute-start.20 = (f32[4,1,16,128]{3,2,1,0:T(8,128)S(1)}, f32[4,1,16,128]{3,2,1,0:T(8,128)}, u32[]{:S(2)}, u32[]{:S(2)}) collective-permute-start(f32[4,1,16,128]{3,2,1,0:T(8,128)S(1)} %get-tuple-element.17), channel_id=1, source_target_pairs={{8,0},{16,8},{24,16},{32,24},{40,32},{48,40},{56,48},{64,56},{72,6... | collective-permute-start | bytes 98312 | tf_op jit(solution)/shard_map/ppermute | solution.py:20
  255.4 54.4 %collective-permute-start.23 = (f32[4,1,16,128]{3,2,1,0:T(8,128)}, f32[4,1,16,128]{3,2,1,0:T(8,128)}, u32[]{:S(2)}, u32[]{:S(2)}) collective-permute-start(f32[4,1,16,128]{3,2,1,0:T(8,128)} %get-tuple-element.14), channel_id=1, source_target_pairs={{0,8},{8,16},{16,24},{24,32},{32,40},{40,48},{48,56},{56,64},{64,7... | collective-permute-start | bytes 98312 | tf_op jit(solution)/shard_map/ppermute | solution.py:19
  255.4 54.4 %collective-permute-start.22 = (f32[4,1,16,128]{3,2,1,0:T(8,128)}, f32[4,1,16,128]{3,2,1,0:T(8,128)}, u32[]{:S(2)}, u32[]{:S(2)}) collective-permute-start(f32[4,1,16,128]{3,2,1,0:T(8,128)} %get-tuple-element.15), channel_id=1, source_target_pairs={{8,0},{16,8},{24,16},{32,24},{40,32},{48,40},{56,48},{64,56},{72,6... | collective-permute-start | bytes 98312 | tf_op jit(solution)/shard_map/ppermute | solution.py:20
  (25 other events, 186.3 us)
Sparse Core Ops, SparseCore 0:
  43.3 82.1 all-gather.16
  128.1 79.9 all-gather.14
  210.7 80.0 all-gather.12
  366.7 78.9 all-gather.10
where the time goes:
time: 464 us; the launch traced here: 455 us
  waiting for transfers between devices  195 us (42%)
  local copies, waits for them, and re-layouts  119 us (26%)
  other arithmetic  68.2 us (15%)
  starting transfers between devices  56.2 us (12%)
  between operations  15.8 us (3%)
    all_gather x3, waiting for transfers between devices, send_forward(): gathered = lax.all_gather(packed[None], 'gx', axis=0, tiled=True)  100 us
    all_gather x1, waiting for transfers between devices, send_back(): gathered = lax.all_gather(packed[None], 'gx', axis=0, tiled=True)  76.1 us
    ppermute x12, starting transfers between devices, extended(): after = lax.ppermute(first, axis, down)  47.8 us
    reduce_sum x1, other arithmetic, coarsen(): return 0.125 * jnp.sum(blocks, axis=(2, 4, 6))  24.2 us
    slice x6, local copies, waits for them, and re-layouts, fine_padded(): faces_z[:, :, :, 0:1]  19.2 us
    add x3, other arithmetic, shards(): fine_state = fine_fields + fraction * fine_rate  18.7 us
    add x1, local copies, waits for them, and re-layouts, shards(): fine_state = fine_fields + fraction * fine_rate  17.4 us
    slice x3, local copies, waits for them, and re-layouts, fine_padded(): faces_z[:, :, :, 1:2]  15.9 us
  transfers between devices with their start and end apart: 28, of which 14 were waited for; matrix products, arithmetic and copies ran while one was open for 26% of the time, Pallas kernels for 0%

commit v1 on v0

v1 whole, which is shorter than its diff:
```python
import functools

import jax
import jax.numpy as jnp
from jax import lax
from jax.experimental import pallas as pl
from jax.experimental.pallas import tpu as pltpu
from jax.sharding import PartitionSpec as P

MESH = pl.DeviceIdType.MESH
F32 = jnp.float32
BF16 = jnp.bfloat16
diffusion = 0.05
section_weights = (1.0 / 3.0, 0.5, 1.0)

RING_X, RING_Z = 4, 8
BOXES = RING_X * RING_Z
FIELDS, CX, FX, NY, LANES = 4, 16, 32, 16, 128
LOW, TOP = 8, 24
PAY = 88
EDGE = 24
CHUNKS = 4
CHUNK_ROWS = 256 // CHUNKS
COPIES = 160


def split_dot(value, weights):
    high = value.astype(BF16)
    rest = value - high.astype(F32)
    mid = rest.astype(BF16)
    low = (rest - mid.astype(F32)).astype(BF16)
    out = jnp.dot(low, weights, preferred_element_type=F32)
    out = out + jnp.dot(mid, weights, preferred_element_type=F32)
    return out + jnp.dot(high, weights, preferred_element_type=F32)


def refine_weights():
    row = lax.broadcasted_iota(jnp.int32, (256, 256), 0)
    col = lax.broadcasted_iota(jnp.int32, (256, 256), 1)
    side, cell, odd = col // 128, (col % 128) // 2, col % 2
    main = (row < 128) & (row // 64 == side)
    near = main & (row % 64 == cell)
    far = main & (row % 64 == cell + 2 * odd - 1)
    extra = row - 128
    corner = (extra >= 0) & (extra < 4) & (extra // 2 == side)
    corner = corner & (col % 128 == jnp.where(extra % 2 == 0, 0, 127))
    return jnp.where(near, 0.75, jnp.where(far | corner, 0.25, 0.0)).astype(BF16)


def average_weights():
    row = lax.broadcasted_iota(jnp.int32, (256, 128), 0)
    col = lax.broadcasted_iota(jnp.int32, (256, 128), 1)
    hit = (row // 128 == col // 64) & ((row % 128) // 2 == col % 64)
    return jnp.where(hit, 0.125, 0.0).astype(BF16)


def interleave_weights():
    row = lax.broadcasted_iota(jnp.int32, (128, 128), 0)
    col = lax.broadcasted_iota(jnp.int32, (128, 128), 1)
    return jnp.where(col == 2 * (row % 64) + row // 64, 1.0, 0.0).astype(BF16)


def coefficients(wind, fraction):
    weight = (0.5 * fraction) * wind
    base = diffusion * fraction
    return base - weight, base + weight


def stepped(state, at, field, base, ghost, coefs, fraction, lane):
    q = state[at, field, LOW:TOP, :]
    behind = state[at - 1, field, LOW:TOP, :]
    ahead = state[at + 1, field, LOW:TOP, :]
    below = state[at, field, LOW - 1 : TOP - 1, :]
    above = state[at, field, LOW + 1 : TOP + 1, :]
    under = pltpu.roll(jnp.where(lane == 127, ghost, q), 1, 1)
    over = pltpu.roll(jnp.where(lane == 0, ghost, q), 127, 1)
    (xp, xm), (yp, ym), (zp, zm) = coefs
    total = (xp * ahead + xm * behind) + (yp * above + ym * below) + (zp * over + zm * under)
    return total + (base - (6.0 * diffusion * fraction) * q)


def kernel(
    cf, cw, ff, fw, own, co, fo,
    sc0, sc1, sc2, sc3, wc, sf0, sf1, sf2, sf3, wf,
    ysend, yrecv, zsend, zrecv, pays, paysel, payzs, slab, corner, face, zt, zface,
    pairs, avg0s, avgzs, result, w_face, w_avg, w_mix,
    send_sem, recv_sem, load_sem,
):
    gx, gy, gz = lax.axis_index("gx"), lax.axis_index("gy"), lax.axis_index("gz")
    tz, tx = gx // RING_X, gx % RING_X

    def along_x(step):
        return (tz * RING_X + (tx + step + RING_X) % RING_X, gy, gz)

    def along_z(step):
        return (((tz + step + RING_Z) % RING_Z) * RING_X + tx, gy, gz)

    def along_row(step):
        return ((gx + step + BOXES) % BOXES, gy, gz)

    def along_y(step):
        return (gx, (gy + step + 4) % 4, gz)

    other_z = (gx, gy, 1 - gz)

    sent = []

    def ship(src, dst, device):
        at = len(sent)
        copy = pltpu.make_async_remote_copy(
            src_ref=src, dst_ref=dst, send_sem=send_sem.at[at], recv_sem=recv_sem.at[at],
            device_id=device, device_id_type=MESH,
        )
        copy.start()
        sent.append(copy)
        return copy

    loads = []

    def load(src, dst):
        copy = pltpu.make_async_copy(src, dst, load_sem.at[len(loads)])
        copy.start()
        loads.append(copy)
        return copy

    in_cf = [load(cf.at[f], sc0.at[pl.ds(1, CX), f, pl.ds(LOW, NY), :]) for f in range(FIELDS)]
    in_ff = [load(ff.at[f], sf0.at[pl.ds(1, FX), f, pl.ds(LOW, NY), :]) for f in range(FIELDS)]
    in_cw = load(cw, wc)
    in_fw = load(fw, wf)

    barrier = pltpu.get_barrier_semaphore()
    partners = [along_x(s) for s in (-1, 1, 2)] + [along_z(s) for s in (-2, -1, 1, 2)]
    partners += [along_row(-1), along_row(1), along_y(-1), along_y(1), other_z]
    for partner in partners:
        pl.semaphore_signal(barrier, inc=1, device_id=partner, device_id_type=MESH)

    lane = lax.broadcasted_iota(jnp.int32, (NY, LANES), 1)
    lane8 = lax.broadcasted_iota(jnp.int32, (8, LANES), 1)
    w_face[...] = refine_weights()
    w_avg[...] = average_weights()
    w_mix[...] = interleave_weights()

    shift = (own[0] - gx + BOXES) % BOXES
    back = (BOXES - shift) % BOXES
    shift_x = shift % RING_X
    shift_z = (shift // RING_X + (tx + shift_x) // RING_X) % RING_Z
    back_x = back % RING_X
    back_z = (back // RING_X + (tx + back_x) // RING_X) % RING_Z

    pl.semaphore_wait(barrier, len(partners))

    coarse = [sc0, sc1, sc2]
    fine = [sf0, sf1, sf2]
    halo = {}

    def coarse_x_halo(k):
        s = coarse[k]
        a = ship(s.at[CX, :, pl.ds(LOW, NY), :], s.at[0, :, pl.ds(LOW, NY), :], along_row(1))
        b = ship(s.at[1, :, pl.ds(LOW, NY), :], s.at[CX + 1, :, pl.ds(LOW, NY), :], along_row(-1))
        halo["cx", k] = (a, b)

    def fine_x_halo(k):
        s = fine[k]
        a = ship(s.at[FX, :, pl.ds(LOW, NY), :], s.at[0, :, pl.ds(LOW, NY), :], along_row(1))
        b = ship(s.at[1, :, pl.ds(LOW, NY), :], s.at[FX + 1, :, pl.ds(LOW, NY), :], along_row(-1))
        halo["fx", k] = (a, b)

    def pack(k):
        s = coarse[k]
        edge_lane = jnp.where(gz == 0, 127, 0)

        def group(g, carry):
            acc_z, acc_t, acc_c = carry
            lows, highs = [], []
            for h in range(2):
                x = 2 * g + h + 1
                ysend[k, 0, g, 4 * h : 4 * h + 4, :] = s[x, :, LOW, :]
                ysend[k, 1, g, 4 * h : 4 * h + 4, :] = s[x, :, TOP - 1, :]
                lows.append(0.75 * s[x, :, LOW + 3, :] + 0.25 * s[x, :, LOW + 4, :])
                highs.append(0.25 * s[x, :, LOW + 11, :] + 0.75 * s[x, :, LOW + 12, :])
                for f in range(FIELDS):
                    p = 8 * g + 4 * h + f
                    q = s[x, f, LOW:TOP, :]
                    moved = pltpu.roll(q, (2 * p + gz - edge_lane + 128) % 128, 1)
                    acc_z = jnp.where(lane == 2 * p + gz, moved, acc_z)
                    after = pltpu.roll(q, 127, 1)
                    t = jnp.where(lane < 64, 0.75 * q + 0.25 * after, 0.25 * q + 0.75 * after)
                    t = pltpu.roll(t, (p - 31 + 128) % 128, 1)
                    acc_t = jnp.where(lane % 64 == p, t, acc_t)
            low = jnp.concatenate(lows, axis=0)
            high = jnp.concatenate(highs, axis=0)
            row = pl.multiple_of(8 * g, 8)
            pays[k][0, pl.ds(row, 8), :] = jnp.where(
                lane8 < 64, pltpu.roll(low, 96, 1), pltpu.roll(high, 32, 1)
            )
            for n, (value, source) in enumerate(((low, 31), (low, 96), (high, 31), (high, 96))):
                moved = pltpu.roll(value, (4 * g + n - source + 128) % 128, 1)
                acc_c = jnp.where(lane8 == 4 * g + n, moved, acc_c)
            return acc_z, acc_t, acc_c

        zero = jnp.zeros((NY, LANES), F32)
        acc_z, acc_t, acc_c = lax.fori_loop(
            0, 8, group, (zero, zero, jnp.zeros((8, LANES), F32))
        )
        zsend[k] = acc_z
        pays[k][0, 64:80, :] = acc_t
        pays[k][0, 80:88, :] = acc_c
        halo["cy", k] = (
            ship(ysend.at[k, 1], yrecv.at[k, 0], along_y(1)),
            ship(ysend.at[k, 0], yrecv.at[k, 1], along_y(-1)),
        )
        halo["cz", k] = (ship(zsend.at[k], zrecv.at[k], other_z),)

    def wait(*names):
        for name in names:
            for copy in halo.pop(name):
                copy.wait_recv()

    def forward_x(k):
        src = pays[k].at[0]
        halo["px", k] = tuple(
            ship(src, pays[k].at[slot], along_x(-slot)) for slot in (1, 2, 3)
        )

    def forward_z1(k):
        wait(("px", k))
        paysel[k] = pays[k][shift_x]
        payzs[k][0] = paysel[k]
        halo["pz1", k] = tuple(
            ship(paysel.at[k], payzs[k].at[slot], along_z(-step))
            for slot, step in ((2, 2), (6, -2), (1, 1), (7, -1))
        )

    def forward_z2(k):
        copies = halo.pop(("pz1", k))
        halo["pz1", k] = copies[2:]
        for copy in copies[:2]:
            copy.wait_recv()
        half = PAY // 2 + 4
        first, second = pl.ds(0, half), pl.ds(half, PAY - half)
        halo["pz2", k] = (
            ship(payzs[k].at[2, first], payzs[k].at[4, first], along_z(-2)),
            ship(payzs[k].at[6, second], payzs[k].at[4, second], along_z(2)),
            ship(payzs[k].at[2], payzs[k].at[3], along_z(-1)),
            ship(payzs[k].at[6], payzs[k].at[5], along_z(1)),
        )

    def arrive(k):
        wait(("pz1", k), ("pz2", k))
        slab[k, 8:72, :] = payzs[k][shift_z, 0:64, :]
        slab[k, 80:104, :] = payzs[k][shift_z, 64:88, :]
        s = slab.at[k]
        halo["edge", k] = (
            ship(s.at[pl.ds(64, 8)], s.at[pl.ds(0, 8)], along_row(1)),
            ship(s.at[pl.ds(80, EDGE)], s.at[pl.ds(104, EDGE)], along_row(1)),
            ship(s.at[pl.ds(8, 8)], s.at[pl.ds(72, 8)], along_row(-1)),
            ship(s.at[pl.ds(80, EDGE)], s.at[pl.ds(128, EDGE)], along_row(-1)),
        )

    def faces(k):
        wait(("edge", k))
        s = slab.at[k]
        cols = s[96:104, :]
        for g in range(8):
            corner[8 + 8 * g : 16 + 8 * g, :] = pltpu.roll(cols, (128 - 4 * g) % 128, 1)
        corner[0:8, :] = pltpu.roll(s[120:128, :], 100, 1)
        corner[72:80, :] = s[144:152, :]
        parts = []
        for ref in (s, corner):
            before, here, after = ref[4:68, :], ref[8:72, :], ref[12:76, :]
            even = 0.25 * before + 0.75 * here
            odd = 0.75 * here + 0.25 * after
            parts.append(jnp.concatenate((even, odd), axis=0))
        wide = jnp.concatenate(parts, axis=1)
        made = split_dot(wide, w_face[...])
        face[...] = made.reshape(16, 8, 256)
        state = fine[k]

        def place(g, carry):
            for o in range(2):
                rows = face[8 * o + g]
                for h in range(2):
                    x = 4 * g + 2 * h + o + 1
                    state[x, :, LOW - 1, :] = rows[4 * h : 4 * h + 4, 0:128]
                    state[x, :, TOP, :] = rows[4 * h : 4 * h + 4, 128:256]
            return carry

        lax.fori_loop(0, 8, place, 0)

        own_z, left, right = s[80:96, :], s[104:120, :], s[128:144, :]
        before = jnp.where(lane % 64 < 4, pltpu.roll(left, 68, 1), pltpu.roll(own_z, 4, 1))
        after = jnp.where(lane % 64 >= 60, pltpu.roll(right, 60, 1), pltpu.roll(own_z, 124, 1))
        zt[0] = 0.25 * before + 0.75 * own_z
        zt[1] = 0.75 * own_z + 0.25 * after
        for o in range(2):
            near = zt[o, 4:12, :]
            zface[o, pl.ds(0, 8, stride=2), :] = 0.25 * zt[o, 3:11, :] + 0.75 * near
            zface[o, pl.ds(1, 8, stride=2), :] = 0.75 * near + 0.25 * zt[o, 5:13, :]
        both = zface[...].reshape(32, LANES)
        zface[...] = split_dot(both, w_mix[...]).reshape(2, NY, LANES)

    def coarse_plane(k, x):
        fraction = section_weights[k]
        s = coarse[k]
        coefs = [coefficients(wc[d, x], fraction) for d in range(3)]
        column = zrecv[k]
        for f in range(FIELDS):
            ghost = pltpu.roll(column, (127 - 2 * (FIELDS * x + f) + 128) % 128, 1)
            base = sc0[x + 1, f, LOW:TOP, :]
            new = stepped(s, x + 1, f, base, ghost, coefs, fraction, lane)
            if k == 2:
                sc3[f, x] = new
            else:
                coarse[k + 1][x + 1, f, LOW:TOP, :] = new

    def coarse_section(k):
        s = coarse[k]
        wait(("cy", k), ("cz", k))

        def place(g, carry):
            for h in range(2):
                s[2 * g + h + 1, :, LOW - 1, :] = yrecv[k, 0, g, 4 * h : 4 * h + 4, :]
                s[2 * g + h + 1, :, TOP, :] = yrecv[k, 1, g, 4 * h : 4 * h + 4, :]
            return carry

        lax.fori_loop(0, 8, place, 0)

        def inner(x, carry):
            coarse_plane(k, x)
            return carry

        lax.fori_loop(1, CX - 1, inner, 0)
        wait(("cx", k))
        coarse_plane(k, jnp.int32(0))
        coarse_plane(k, jnp.int32(CX - 1))
        if k < 2:
            coarse_x_halo(k + 1)

    def fine_plane(k, j, o):
        fraction = section_weights[k]
        s = fine[k]
        x = 2 * j + o
        coefs = [coefficients(wf[d, x], fraction) for d in range(3)]
        column = zface[o]
        made = []
        for f in range(FIELDS):
            ghost = pltpu.roll(column, (127 - 2 * (FIELDS * j + f) + 128) % 128, 1)
            base = sf0[x + 1, f, LOW:TOP, :]
            new = stepped(s, x + 1, f, base, ghost, coefs, fraction, lane)
            made.append(new)
            if k == 2:
                sf3[f, x] = new
            else:
                fine[k + 1][x + 1, f, LOW:TOP, :] = new
        return made

    def fine_section(k):
        wait(("fx", k))

        def pair(j, carry):
            fine_plane(k, j, 0)
            fine_plane(k, j, 1)
            return carry

        pair(jnp.int32(0), 0)
        pair(jnp.int32(15), 0)
        fine_x_halo(k + 1)
        lax.fori_loop(1, 15, pair, 0)

    def last_section():
        wait(("fx", 2))

        def pair(j, carry):
            first = fine_plane(2, j, 0)
            second = fine_plane(2, j, 1)
            for f in range(FIELDS):
                pairs[j, f] = first[f] + second[f]
            return carry

        for c in range(CHUNKS):
            j0 = c * (16 // CHUNKS)
            lax.fori_loop(j0, j0 + 16 // CHUNKS, pair, 0)
            rows = []
            for j in range(j0, j0 + 16 // CHUNKS):
                for fp in range(2):
                    halves = [
                        pairs[j, 2 * fp + n, pl.ds(0, 8, stride=2), :]
                        + pairs[j, 2 * fp + n, pl.ds(1, 8, stride=2), :]
                        for n in range(2)
                    ]
                    rows.append(jnp.concatenate(halves, axis=1))
            avg0s[c][0] = split_dot(jnp.concatenate(rows, axis=0), w_avg[...])
            src = avg0s[c].at[0]
            halo["ax1", c] = (
                ship(src, avg0s[c].at[3], along_x(1)),
                ship(src, avg0s[c].at[1], along_x(-1)),
            )

    def average_x2(c):
        wait(("ax1", c))
        first, second = pl.ds(0, CHUNK_ROWS // 2), pl.ds(CHUNK_ROWS // 2, CHUNK_ROWS // 2)
        halo["ax2", c] = (
            ship(avg0s[c].at[3, first], avg0s[c].at[2, first], along_x(1)),
            ship(avg0s[c].at[1, second], avg0s[c].at[2, second], along_x(-1)),
        )

    def average_z(c, step):
        if step == 1:
            wait(("ax2", c))
            avgzs[c][0] = avg0s[c][back_x]
        else:
            wait(("az", c, step - 1))
        up, down = (RING_Z - step + 1) % RING_Z, step - 1
        if step < 4:
            halo["az", c, step] = (
                ship(avgzs[c].at[up], avgzs[c].at[up - 1 if up else 7], along_z(1)),
                ship(avgzs[c].at[down], avgzs[c].at[down + 1], along_z(-1)),
            )
        else:
            half = CHUNK_ROWS // 2
            first, second = pl.ds(0, half), pl.ds(half, half)
            halo["az", c, step] = (
                ship(avgzs[c].at[5, first], avgzs[c].at[4, first], along_z(1)),
                ship(avgzs[c].at[3, second], avgzs[c].at[4, second], along_z(-1)),
            )

    inside = (lane8 >= 32) & (lane8 < 96)

    def average_done(c):
        wait(("az", c, 4))
        result[...] = avgzs[c][back_z].reshape(CHUNK_ROWS // 8, 8, LANES)
        for j in range(16 // CHUNKS):
            x = c * (16 // CHUNKS) + j
            for fp in range(2):
                block = result[2 * j + fp]
                for n in range(2):
                    f = 2 * fp + n
                    moved = pltpu.roll(block, 32 if n == 0 else 96, 1)
                    sc3[f, x, 4:12, :] = jnp.where(inside, moved, sc3[f, x, 4:12, :])

    for copy in in_cf:
        copy.wait()
    coarse_x_halo(0)
    pack(0)
    forward_x(0)
    for copy in in_ff:
        copy.wait()
    fine_x_halo(0)
    in_cw.wait()
    coarse_section(0)
    pack(1)
    forward_x(1)
    forward_z1(0)
    coarse_section(1)
    pack(2)
    forward_x(2)
    forward_z2(0)
    forward_z1(1)
    arrive(0)
    forward_z1(2)
    forward_z2(1)
    in_fw.wait()
    faces(0)
    fine_section(0)
    forward_z2(2)
    arrive(1)
    coarse_section(2)
    faces(1)
    fine_section(1)
    arrive(2)
    faces(2)
    last_section()
    out_fine = load(sf3, fo)
    for c in range(CHUNKS):
        average_x2(c)
    for step in (1, 2, 3, 4):
        for c in range(CHUNKS):
            average_z(c, step)
    for c in range(CHUNKS):
        average_done(c)
    out_coarse = load(sc3, co)
    for copy in sent:
        copy.wait_send()
    out_fine.wait()
    out_coarse.wait()


def shards(coarse_fields, coarse_wind, fine_fields, fine_wind, fine_owner):
    anywhere = pl.BlockSpec(memory_space=pl.ANY)
    vmem = lambda *shape: pltpu.VMEM(shape, F32)
    scratch = (
        [vmem(CX + 2, FIELDS, 32, LANES)] * 3
        + [vmem(FIELDS, CX, NY, LANES), vmem(3, CX, NY, LANES)]
        + [vmem(FX + 2, FIELDS, 32, LANES)] * 3
        + [vmem(FIELDS, FX, NY, LANES), vmem(3, FX, NY, LANES)]
        + [
            vmem(3, 2, 8, 8, LANES), vmem(3, 2, 8, 8, LANES),
            vmem(3, NY, LANES), vmem(3, NY, LANES),
            [vmem(RING_X, PAY, LANES)] * 3, vmem(3, PAY, LANES), [vmem(RING_Z, PAY, LANES)] * 3,
            vmem(3, 152, LANES), vmem(80, LANES), vmem(16, 8, 256),
            vmem(2, NY, LANES), vmem(2, NY, LANES),
            vmem(CX, FIELDS, NY, LANES),
            [vmem(RING_X, CHUNK_ROWS, LANES)] * CHUNKS,
            [vmem(RING_Z, CHUNK_ROWS, LANES)] * CHUNKS,
            vmem(CHUNK_ROWS // 8, 8, LANES),
            pltpu.VMEM((256, 256), BF16), pltpu.VMEM((256, 128), BF16),
            pltpu.VMEM((128, 128), BF16),
            pltpu.SemaphoreType.DMA((COPIES,)), pltpu.SemaphoreType.DMA((COPIES,)),
            pltpu.SemaphoreType.DMA((16,)),
        ]
    )
    return pl.pallas_call(
        kernel,
        out_shape=(
            jax.ShapeDtypeStruct(coarse_fields.shape, F32),
            jax.ShapeDtypeStruct(fine_fields.shape, F32),
        ),
        in_specs=[anywhere] * 4 + [pl.BlockSpec(memory_space=pltpu.SMEM)],
        out_specs=(anywhere, anywhere),
        scratch_shapes=scratch,
        compiler_params=pltpu.CompilerParams(
            collective_id=0, has_side_effects=True, vmem_limit_bytes=48 * 1024 * 1024
        ),
        name="two_level_step",
    )(coarse_fields, coarse_wind, fine_fields, fine_wind, fine_owner.reshape((1,)))


def solution(mesh):
    spec = P(None, "gx", "gy", "gz")
    return jax.shard_map(
        shards,
        mesh=mesh,
        in_specs=(spec, spec, spec, spec, P("gx", "gy", "gz")),
        out_specs=(spec, spec),
        check_vma=False,
    )
```

time: 464 us -> 86.9 us (0.19); the launches traced: 455 us -> 85.3 us
  waiting for transfers between devices: 195 us -> 0 us
  local copies, waits for them, and re-layouts: 119 us -> 6.15 us
  Pallas kernels: 0 us -> 77.9 us
  other arithmetic: 68.2 us -> 0 us
  starting transfers between devices: 56.2 us -> 0 us
  between operations: 15.8 us -> 1.3 us
    all_gather x4 -> x0, waiting for transfers between devices: 176 us -> none  [the longest x3 100 us: send_forward(): gathered = lax.all_gather(packed[None], 'gx', axis=0, tiled=True)]
    pallas_call x0 -> x1, Pallas kernels: none -> 77.9 us  [shards(): pl.pallas_call(kernel, out_shape=(jax.ShapeDtypeStruct(coarse_fields.shap...]
    slice x58 -> x0, local copies, waits for them, and re-layouts: 58.9 us -> none  [the longest x6 19.2 us: fine_padded(): faces_z[:, :, :, 0:1]]
    ppermute x24 -> x0, starting transfers between devices: 55.7 us -> none  [the longest x12 47.8 us: extended(): after = lax.ppermute(first, axis, down)]
    add x12 -> x0, other arithmetic: 25.3 us -> none  [the longest x3 18.7 us: shards(): fine_state = fine_fields + fraction * fine_rate]
    reduce_sum x1 -> x0, other arithmetic: 24.2 us -> none  [coarsen(): return 0.125 * jnp.sum(blocks, axis=(2, 4, 6))]
    ppermute x24 -> x0, waiting for transfers between devices: 19 us -> none  [the longest x12 15.6 us: extended(): before = lax.ppermute(last, axis, up)]
    add x1 -> x0, local copies, waits for them, and re-layouts: 17.4 us -> none  [shards(): fine_state = fine_fields + fraction * fine_rate]
  transfers between devices with their start and end apart: 28 -> 0, of which waited for: 14 -> 0; matrix products, arithmetic and copies ran while one was open for 26% -> 0% of each run, Pallas kernels for 0% -> 0%
where the time goes in v1:
time: 86.9 us; the launch traced here: 85.3 us
  Pallas kernels  77.9 us (90%)
  local copies, waits for them, and re-layouts  6.15 us (7%)
  between operations  1.3 us (1%)
    pallas_call x1, Pallas kernels, shards(): pl.pallas_call(kernel, out_shape=(jax.ShapeDtypeStruct(coarse_fields.shap...  77.9 us
    unnamed x10, local copies, waits for them, and re-layouts  6.15 us

profile of v1, /device:TPU:24, one launch (start us, length us, event | category | flops | bytes accessed | tf_op | source)
XLA Modules:
  0.0 85.3 jit_solution(10975268529526584317)
XLA Ops:
  1.3 0.0 copy-start
  1.3 1.2 %copy-done = f32[4,32,16,128]{3,2,1,0:T(8,128)S(1)} copy-done((f32[4,32,16,128]{3,2,1,0:T(8,128)S(1)}, f32[4,32,16,128]{3,2,1,0:T(8,128)}, u32[]{:S(2)}) %copy-start) | copy-done | bytes 1048600
  2.5 0.0 copy-start.1
  2.5 1.1 %copy-done.1 = f32[3,32,16,128]{3,2,1,0:T(8,128)S(1)} copy-done((f32[3,32,16,128]{3,2,1,0:T(8,128)S(1)}, f32[3,32,16,128]{3,2,1,0:T(8,128)}, u32[]{:S(2)}) %copy-start.1) | copy-done | bytes 786456
  3.6 0.0 copy-start.2
  3.6 1.0 %copy-done.2 = f32[4,16,16,128]{3,2,1,0:T(8,128)S(1)} copy-done((f32[4,16,16,128]{3,2,1,0:T(8,128)S(1)}, f32[4,16,16,128]{3,2,1,0:T(8,128)}, u32[]{:S(2)}) %copy-start.2) | copy-done | bytes 524312
  4.7 0.0 copy-start.3
  4.7 1.0 %copy-done.3 = f32[3,16,16,128]{3,2,1,0:T(8,128)S(1)} copy-done((f32[3,16,16,128]{3,2,1,0:T(8,128)S(1)}, f32[3,16,16,128]{3,2,1,0:T(8,128)}, u32[]{:S(2)}) %copy-start.3) | copy-done | bytes 393240
  5.7 77.9 %two_level_step.1 = (f32[4,16,16,128]{3,2,1,0:T(8,128)S(1)}, f32[4,32,16,128]{3,2,1,0:T(8,128)S(1)}) custom-call(f32[4,16,16,128]{3,2,1,0:T(8,128)S(1)} %copy-done.2, f32[3,16,16,128]{3,2,1,0:T(8,128)S(1)} %copy-done.3, f32[4,32,16,128]{3,2,1,0:T(8,128)S(1)} %copy-done, f32[3,32,16,128]{3,2,1,0:T(8,128)S(1)} %copy-done.1, s32[1]{0:T(128)} %bitcast.1.own), custom_call_target="tpu_custom_call" | custom-call | tf_op jit(solution)/shard_map/two_level_step/pallas_call | solution.py:512
  83.5 0.8 copy.10
  84.3 1.0 %copy.11 = f32[4,32,16,128]{3,2,1,0:T(8,128)} copy(f32[4,32,16,128]{3,2,1,0:T(8,128)S(1)} %get-tuple-element.5) | data formatting | bytes 2097152
Async XLA Ops:
  1.3 1.2 %copy-start = (f32[4,32,16,128]{3,2,1,0:T(8,128)S(1)}, f32[4,32,16,128]{3,2,1,0:T(8,128)}, u32[]{:S(2)}) copy-start(f32[4,32,16,128]{3,2,1,0:T(8,128)} %ff.1) | copy-start | bytes 3145732
  2.5 1.1 %copy-start.1 = (f32[3,32,16,128]{3,2,1,0:T(8,128)S(1)}, f32[3,32,16,128]{3,2,1,0:T(8,128)}, u32[]{:S(2)}) copy-start(f32[3,32,16,128]{3,2,1,0:T(8,128)} %fw.1) | copy-start | bytes 2359300
  3.6 1.0 %copy-start.2 = (f32[4,16,16,128]{3,2,1,0:T(8,128)S(1)}, f32[4,16,16,128]{3,2,1,0:T(8,128)}, u32[]{:S(2)}) copy-start(f32[4,16,16,128]{3,2,1,0:T(8,128)} %cf.1) | copy-start | bytes 1572868
  4.7 1.0 %copy-start.3 = (f32[3,16,16,128]{3,2,1,0:T(8,128)S(1)}, f32[3,16,16,128]{3,2,1,0:T(8,128)}, u32[]{:S(2)}) copy-start(f32[3,16,16,128]{3,2,1,0:T(8,128)} %cw.1) | copy-start | bytes 1179652

commit v2 on v1

v2 whole, which is shorter than its diff:
```python
import functools

import jax
import jax.numpy as jnp
from jax import lax
from jax.experimental import pallas as pl
from jax.experimental.pallas import tpu as pltpu
from jax.sharding import PartitionSpec as P

MESH = pl.DeviceIdType.MESH
F32 = jnp.float32
BF16 = jnp.bfloat16
diffusion = 0.05
section_weights = (1.0 / 3.0, 0.5, 1.0)

RING_X, RING_Z = 4, 8
BOXES = RING_X * RING_Z
FIELDS, CX, FX, NY, LANES = 4, 16, 32, 16, 128
LOW, TOP = 8, 24
PAY = 104
CHUNKS = 4
CHUNK_ROWS = 256 // CHUNKS
COPIES = 72
STRIDES = (1, 3)


def split_dot(value, weights):
    high = value.astype(BF16)
    rest = value - high.astype(F32)
    mid = rest.astype(BF16)
    low = (rest - mid.astype(F32)).astype(BF16)
    out = jnp.dot(low, weights, preferred_element_type=F32)
    out = out + jnp.dot(mid, weights, preferred_element_type=F32)
    return out + jnp.dot(high, weights, preferred_element_type=F32)


def refine_weights():
    row = lax.broadcasted_iota(jnp.int32, (256, 256), 0)
    col = lax.broadcasted_iota(jnp.int32, (256, 256), 1)
    side, cell, odd = col // 128, (col % 128) // 2, col % 2
    main = (row < 128) & (row // 64 == side)
    near = main & (row % 64 == cell)
    far = main & (row % 64 == cell + 2 * odd - 1)
    extra = row - 128
    corner = (extra >= 0) & (extra < 4) & (extra // 2 == side)
    corner = corner & (col % 128 == jnp.where(extra % 2 == 0, 0, 127))
    return jnp.where(near, 0.75, jnp.where(far | corner, 0.25, 0.0)).astype(BF16)


def average_weights():
    row = lax.broadcasted_iota(jnp.int32, (256, 128), 0)
    col = lax.broadcasted_iota(jnp.int32, (256, 128), 1)
    hit = (row // 128 == col // 64) & ((row % 128) // 2 == col % 64)
    return jnp.where(hit, 0.125, 0.0).astype(BF16)


def interleave_weights():
    row = lax.broadcasted_iota(jnp.int32, (256, 256), 0)
    col = lax.broadcasted_iota(jnp.int32, (256, 256), 1)
    side, p = row // 128, row % 128
    inner = (p >= 8) & (p < 72) & (col == 2 * (p - 8) + side)
    before = (p >= 4) & (p < 8) & (col == 128 + 2 * (p - 4) + side)
    after = (p >= 72) & (p < 76) & (col == 136 + 2 * (p - 72) + side)
    return jnp.where(inner | before | after, 1.0, 0.0).astype(BF16)


def coefficients(wind, fraction):
    weight = (0.5 * fraction) * wind
    base = diffusion * fraction
    return base - weight, base + weight


def stepped(state, field, at, base, ghost, coefs, fraction, lane):
    q = state[field, at, LOW:TOP, :]
    behind = state[field, at - 1, LOW:TOP, :]
    ahead = state[field, at + 1, LOW:TOP, :]
    below = state[field, at, LOW - 1 : TOP - 1, :]
    above = state[field, at, LOW + 1 : TOP + 1, :]
    low_side = q if ghost is None else jnp.where(lane == 127, ghost, q)
    top_side = q if ghost is None else jnp.where(lane == 0, ghost, q)
    under = pltpu.roll(low_side, 1, 1)
    over = pltpu.roll(top_side, 127, 1)
    (xp, xm), (yp, ym), (zp, zm) = coefs
    total = (xp * ahead + xm * behind) + (yp * above + ym * below) + (zp * over + zm * under)
    return total + (base - (6.0 * diffusion * fraction) * q)


def kernel(
    cf, cw, ff, fw, own, co, fo,
    tc0, tc1, tc2, uc1, uc2, sc3, wc, sf0, sf1, sf2, sf3, wf,
    ysend, yrecv, zsend, zrecv, payxs, payzs, slab, corner, face, zt, zface,
    pairs, avgxs, avgzs, result, w_face, w_avg, w_mix,
    send_sem, recv_sem, load_sem,
):
    gx, gy, gz = lax.axis_index("gx"), lax.axis_index("gy"), lax.axis_index("gz")
    tz, tx = gx // RING_X, gx % RING_X

    def along_x(step):
        return (tz * RING_X + (tx + step + RING_X) % RING_X, gy, gz)

    def along_z(step):
        return (((tz + step + RING_Z) % RING_Z) * RING_X + tx, gy, gz)

    def along_row(step):
        return ((gx + step + BOXES) % BOXES, gy, gz)

    def along_y(step):
        return (gx, (gy + step + 4) % 4, gz)

    other_z = (gx, gy, 1 - gz)

    sent = []
    halo = {}

    def ship(src, dst, device):
        at = len(sent)
        copy = pltpu.make_async_remote_copy(
            src_ref=src, dst_ref=dst, send_sem=send_sem.at[at], recv_sem=recv_sem.at[at],
            device_id=device, device_id_type=MESH,
        )
        copy.start()
        sent.append(copy)
        return copy

    def wait(*names):
        for name in names:
            for copy in halo.pop(name):
                copy.wait_recv()

    loads = []

    def load(src, dst):
        copy = pltpu.make_async_copy(src, dst, load_sem.at[len(loads)])
        copy.start()
        loads.append(copy)
        return copy

    rows = pl.ds(LOW, NY)
    in_cf = load(cf, tc0.at[:, pl.ds(3, CX), rows, :])
    in_cw = load(cw, wc.at[:, pl.ds(2, CX)])
    in_ff = load(ff, sf0.at[:, pl.ds(3, FX), rows, :])
    in_fw = load(fw, wf.at[:, pl.ds(2, FX)])

    barrier = pltpu.get_barrier_semaphore()
    partners = [along_row(-1), along_row(1), along_y(-1), along_y(1), other_z]
    partners += [along_x(s) for s in (-1, 1, 2)] + [along_z(s) for s in (-3, -1, 1, 3)]
    for partner in partners:
        pl.semaphore_signal(barrier, inc=1, device_id=partner, device_id_type=MESH)

    lane = lax.broadcasted_iota(jnp.int32, (NY, LANES), 1)
    lane8 = lax.broadcasted_iota(jnp.int32, (8, LANES), 1)

    def parts_of(shift):
        part_x = shift % RING_X
        part_z = (shift // RING_X + (tx + part_x) // RING_X) % RING_Z
        signed = part_z - jnp.where(part_z > 4, RING_Z, 0)
        third = (signed + 4) // 3
        return part_x, signed - 3 * third + 4, third

    shift = (own[0] - gx + BOXES) % BOXES
    there = parts_of(shift)
    home = parts_of((BOXES - shift) % BOXES)

    def start_halos():
        def both(name, src, dst, first, last, width, end, where):
            halo[name] = (
                ship(src.at[:, pl.ds(last, width)], where(dst, 0, width), along_row(1)),
                ship(src.at[:, pl.ds(first, width)], where(dst, end, width), along_row(-1)),
            )

        padded = lambda ref, at, width: ref.at[:, pl.ds(at, width), rows, :]
        plain = lambda ref, at, width: ref.at[:, pl.ds(at, width)]
        both("cf", cf, tc0, 0, CX - 3, 3, CX + 3, padded)
        both("cw", cw, wc, 0, CX - 2, 2, CX + 2, plain)
        both("ff", ff, sf0, 0, FX - 3, 3, FX + 3, padded)
        both("fw", fw, wf, 0, FX - 2, 2, FX + 2, plain)

    slabs = [tc0, tc1, tc2]

    def slab_range(k, first, last):
        fraction = section_weights[k]

        def inner(at, carry):
            coefs = [coefficients(wc[d, at - 1], fraction) for d in range(3)]
            for f in range(FIELDS):
                base = tc0[f, at, rows, :]
                new = stepped(slabs[k], f, at, base, None, coefs, fraction, lane)
                slabs[k + 1][f, at, rows, :] = new
            return carry

        lax.fori_loop(first + 3, last + 3, inner, 0)

    def pack_start():
        zero = jnp.zeros((NY, LANES), F32)
        return zero, zero, jnp.zeros((8, LANES), F32)

    def pack_group(k, g, carry):
        s = slabs[k]
        low_z, high_z, ends = carry
        lows, highs = [], []
        for h in range(2):
            at = 2 * g + h + 1
            lows.append(0.75 * s[:, at, LOW + 3, :] + 0.25 * s[:, at, LOW + 4, :])
            highs.append(0.25 * s[:, at, LOW + 11, :] + 0.75 * s[:, at, LOW + 12, :])
            for f in range(FIELDS):
                p = 8 * g + 4 * h + f
                q = s[f, at, rows, :]
                after = pltpu.roll(q, 127, 1)
                t = jnp.where(lane < 64, 0.75 * q + 0.25 * after, 0.25 * q + 0.75 * after)
                low_z = jnp.where(lane == p, pltpu.roll(t, (p - 31 + 128) % 128, 1), low_z)
                high_z = jnp.where(lane == p, pltpu.roll(t, (p - 95 + 128) % 128, 1), high_z)
        low = jnp.concatenate(lows, axis=0)
        high = jnp.concatenate(highs, axis=0)
        row = pl.multiple_of(8 * g, 8)
        payxs[k][0, pl.ds(row, 8), :] = jnp.where(
            lane8 < 64, pltpu.roll(low, 96, 1), pltpu.roll(high, 32, 1)
        )
        for n, (value, source) in enumerate(((low, 31), (low, 96), (high, 31), (high, 96))):
            to = 80 + 4 * g + n
            ends = jnp.where(lane8 == to, pltpu.roll(value, (to - source + 128) % 128, 1), ends)
        return low_z, high_z, ends

    def pack_range(k, first, last, carry):
        return lax.fori_loop(first, last, functools.partial(pack_group, k), carry)

    def pack_end(k, carry):
        low_z, high_z, ends = carry
        payxs[k][0, 80:88, :] = jnp.where(lane8 >= 80, ends, low_z[3:11, :])
        payxs[k][0, 88:90, :] = low_z[11:13, :]
        payxs[k][0, 92:102, :] = high_z[3:13, :]

    def shift_x(name, bufs):
        halo[name, 0] = tuple(
            ship(bufs.at[0], bufs.at[slot], along_x(-slot)) for slot in (1, 2, 3)
        )

    def faces(k):
        wait((("pay", k), 2))
        slab[...] = payzs[k][1][there[2]]
        cols = slab[80:88, :]
        for g in range(10):
            corner[8 * g : 8 * g + 8, :] = pltpu.roll(cols, (48 - 4 * g + 128) % 128, 1)
        parts = []
        for ref in (slab, corner):
            before, here, after = ref[0:72, :], ref[4:76, :], ref[8:80, :]
            even = 0.25 * before + 0.75 * here
            odd = 0.75 * here + 0.25 * after
            parts.append(jnp.concatenate((even, odd), axis=0))
        made = split_dot(jnp.concatenate(parts, axis=1), w_face[...])
        face[...] = made.reshape(18, 8, 256)
        state = fine[k]

        def place(m, carry):
            for o in range(2):
                block = face[9 * o + m]
                for h in range(2):
                    at = 4 * m + 2 * h + o + 1
                    state[:, at, LOW - 1, :] = block[4 * h : 4 * h + 4, 0:128]
                    state[:, at, TOP, :] = block[4 * h : 4 * h + 4, 128:256]
            return carry

        lax.fori_loop(0, 9, place, 0)

        for side, first in enumerate((80, 92)):
            v = slab[first : first + 10, :]
            even = 0.25 * pltpu.roll(v, 4, 1) + 0.75 * v
            odd = 0.75 * v + 0.25 * pltpu.roll(v, 124, 1)
            for o, w in enumerate((even, odd)):
                near = 0.75 * w[1:9, :]
                zt[o, side, pl.ds(0, 8, stride=2), :] = 0.25 * w[0:8, :] + near
                zt[o, side, pl.ds(1, 8, stride=2), :] = near + 0.25 * w[2:10, :]
        both = jnp.concatenate(
            [jnp.concatenate((zt[o, 0], zt[o, 1]), axis=1) for o in range(2)], axis=0
        )
        zface[...] = split_dot(both, w_mix[...]).reshape(2, NY, 256)

    def send_edges(k):
        s, off = ((tc0, 3), (uc1, 1), (uc2, 1))[k]
        edge_lane = jnp.where(gz == 0, 127, 0)

        def group(g, acc):
            for h in range(2):
                at = 2 * g + h + off
                ysend[k, 0, g, 4 * h : 4 * h + 4, :] = s[:, at, LOW, :]
                ysend[k, 1, g, 4 * h : 4 * h + 4, :] = s[:, at, TOP - 1, :]
                for f in range(FIELDS):
                    to = 2 * (8 * g + 4 * h + f) + gz
                    moved = pltpu.roll(s[f, at, rows, :], (to - edge_lane + 128) % 128, 1)
                    acc = jnp.where(lane == to, moved, acc)
            return acc

        zsend[k] = lax.fori_loop(0, 8, group, jnp.zeros((NY, LANES), F32))
        copies = [
            ship(ysend.at[k, 1], yrecv.at[k, 0], along_y(1)),
            ship(ysend.at[k, 0], yrecv.at[k, 1], along_y(-1)),
            ship(zsend.at[k], zrecv.at[k], other_z),
        ]
        if k:
            copies += [
                ship(s.at[:, CX, rows, :], s.at[:, 0, rows, :], along_row(1)),
                ship(s.at[:, 1, rows, :], s.at[:, CX + 1, rows, :], along_row(-1)),
            ]
        halo["edges", k] = copies

    def coarse_section(k):
        s, off = ((tc0, 3), (uc1, 1), (uc2, 1))[k]
        fraction = section_weights[k]
        wait(("edges", k))

        def place(g, carry):
            for h in range(2):
                at = 2 * g + h + off
                s[:, at, LOW - 1, :] = yrecv[k, 0, g, 4 * h : 4 * h + 4, :]
                s[:, at, TOP, :] = yrecv[k, 1, g, 4 * h : 4 * h + 4, :]
            return carry

        lax.fori_loop(0, 8, place, 0)
        column = zrecv[k]

        def plane(x, carry):
            coefs = [coefficients(wc[d, x + 2], fraction) for d in range(3)]
            for f in range(FIELDS):
                ghost = pltpu.roll(column, (127 - 2 * (FIELDS * x + f) + 128) % 128, 1)
                base = tc0[f, x + 3, rows, :]
                new = stepped(s, f, x + off, base, ghost, coefs, fraction, lane)
                if k == 2:
                    sc3[f, x] = new
                else:
                    (uc1, uc2)[k][f, x + 1, rows, :] = new
            return carry

        lax.fori_loop(0, CX, plane, 0)

    fine = [sf0, sf1, sf2]

    def fine_plane(k, x, o, half, first):
        fraction = section_weights[k]
        coefs = [coefficients(wf[d, x + 2], fraction) for d in range(3)]
        column = zface[o, :, 128 * half : 128 * half + 128]
        made = []
        for f in range(FIELDS):
            ghost = pltpu.roll(column, (127 - first - 2 * f + 128) % 128, 1)
            base = sf0[f, x + 3, rows, :]
            new = stepped(fine[k], f, x + 3, base, ghost, coefs, fraction, lane)
            made.append(new)
            if k == 2:
                sf3[f, x] = new
            else:
                fine[k + 1][f, x + 3, rows, :] = new
        return made

    def fine_section(k):
        def pair(j, carry):
            fine_plane(k, 2 * j, 0, 0, 8 * j)
            fine_plane(k, 2 * j + 1, 1, 0, 8 * j)
            return carry

        lax.fori_loop(0, 16, pair, 0)
        fine_plane(k, -1, 1, 1, 0)
        fine_plane(k, FX, 0, 1, 8)
        if k == 0:
            fine_plane(k, -2, 0, 1, 0)
            fine_plane(k, FX + 1, 1, 1, 8)

    per = 16 // CHUNKS

    def last_section():
        def pair(j, carry):
            first = fine_plane(2, 2 * j, 0, 0, 8 * j)
            second = fine_plane(2, 2 * j + 1, 1, 0, 8 * j)
            for f in range(FIELDS):
                pairs[j, f] = first[f] + second[f]
            return carry

        for c in range(CHUNKS):
            lax.fori_loop(c * per, (c + 1) * per, pair, 0)
            blocks = []
            for j in range(c * per, (c + 1) * per):
                for fp in range(2):
                    halves = [
                        pairs[j, 2 * fp + n, pl.ds(0, 8, stride=2), :]
                        + pairs[j, 2 * fp + n, pl.ds(1, 8, stride=2), :]
                        for n in range(2)
                    ]
                    blocks.append(jnp.concatenate(halves, axis=1))
            avgxs[c][0] = split_dot(jnp.concatenate(blocks, axis=0), w_avg[...])
            shift_x(("avg", c), avgxs[c])

    inside = (lane8 >= 32) & (lane8 < 96)

    def merge(c):
        wait((("avg", c), 2))
        result[...] = avgzs[c][1][home[2]].reshape(CHUNK_ROWS // 8, 8, LANES)
        for j in range(per):
            x = c * per + j
            for fp in range(2):
                block = result[2 * j + fp]
                for n in range(2):
                    f = 2 * fp + n
                    moved = pltpu.roll(block, 32 if n == 0 else 96, 1)
                    sc3[f, x, 4:12, :] = jnp.where(inside, moved, sc3[f, x, 4:12, :])

    def pay_z(k, turn):
        source = payxs[k] if turn == 0 else payzs[k][0]
        round_z(("pay", k), turn, source, payzs[k][turn], there)

    def avg_z(c, turn):
        source = avgxs[c] if turn == 0 else avgzs[c][0]
        round_z(("avg", c), turn, source, avgzs[c][turn], home)

    def round_z(name, turn, source, bufs, choice):
        wait((name, turn))
        bufs[1] = source[choice[turn]]
        stride = STRIDES[turn]
        halo[name, turn + 1] = tuple(
            ship(bufs.at[1], bufs.at[slot], along_z(step))
            for slot, step in ((0, stride), (2, -stride))
        )

    pl.semaphore_wait(barrier, len(partners))
    start_halos()
    in_cf.wait()
    send_edges(0)
    in_cw.wait()
    slab_range(0, 1, CX - 1)
    slab_range(1, 2, CX - 2)
    packs = [pack_range(0, 1, 9, pack_start())]
    packs += [pack_range(k, 2, 8, pack_start()) for k in (1, 2)]
    for at in (1, CX + 4):
        tc2[:, at, rows, :] = jnp.zeros((FIELDS, NY, LANES), F32)
    wait("cf")
    packs[0] = pack_range(0, 0, 1, packs[0])
    pack_end(0, pack_range(0, 9, 10, packs[0]))
    shift_x(("pay", 0), payxs[0])
    wait("cw")
    slab_range(0, -2, 1)
    slab_range(0, CX - 1, CX + 2)
    packs[1] = pack_range(1, 0, 2, packs[1])
    pack_end(1, pack_range(1, 8, 10, packs[1]))
    shift_x(("pay", 1), payxs[1])
    slab_range(1, -1, 2)
    slab_range(1, CX - 2, CX + 1)
    packs[2] = pack_range(2, 0, 2, packs[2])
    pack_end(2, pack_range(2, 8, 10, packs[2]))
    shift_x(("pay", 2), payxs[2])
    w_face[...] = refine_weights()
    w_avg[...] = average_weights()
    w_mix[...] = interleave_weights()
    coarse_section(0)
    send_edges(1)
    for k in range(3):
        pay_z(k, 0)
    pay_z(0, 1)
    coarse_section(1)
    send_edges(2)
    for k in (1, 2):
        pay_z(k, 1)
    in_ff.wait()
    in_fw.wait()
    wait("ff", "fw")
    faces(0)
    fine_section(0)
    faces(1)
    fine_section(1)
    faces(2)
    last_section()
    out_fine = load(sf3, fo)
    coarse_section(2)
    for turn in range(2):
        for c in range(CHUNKS):
            avg_z(c, turn)
    for c in range(CHUNKS):
        merge(c)
    out_coarse = load(sc3, co)
    for copy in sent:
        copy.wait_send()
    out_fine.wait()
    out_coarse.wait()


def shards(coarse_fields, coarse_wind, fine_fields, fine_wind, fine_owner):
    anywhere = pl.BlockSpec(memory_space=pltpu.HBM)
    vmem = lambda *shape: pltpu.VMEM(shape, F32)
    scratch = (
        [vmem(FIELDS, CX + 6, 32, LANES)] * 3
        + [vmem(FIELDS, CX + 2, 32, LANES)] * 2
        + [vmem(FIELDS, CX, NY, LANES), vmem(3, CX + 4, NY, LANES)]
        + [vmem(FIELDS, FX + 6, 32, LANES)] * 3
        + [vmem(FIELDS, FX, NY, LANES), vmem(3, FX + 4, NY, LANES)]
        + [
            vmem(3, 2, 8, 8, LANES), vmem(3, 2, 8, 8, LANES),
            vmem(3, NY, LANES), vmem(3, NY, LANES),
            [vmem(RING_X, PAY, LANES)] * 3, [[vmem(3, PAY, LANES)] * 2] * 3,
            vmem(PAY, LANES), vmem(80, LANES), vmem(18, 8, 256),
            vmem(2, 2, NY, LANES), vmem(2, NY, 256),
            vmem(CX, FIELDS, NY, LANES),
            [vmem(RING_X, CHUNK_ROWS, LANES)] * CHUNKS,
            [[vmem(3, CHUNK_ROWS, LANES)] * 2] * CHUNKS,
            vmem(CHUNK_ROWS // 8, 8, LANES),
            pltpu.VMEM((256, 256), BF16), pltpu.VMEM((256, 128), BF16),
            pltpu.VMEM((256, 256), BF16),
            pltpu.SemaphoreType.DMA((COPIES,)), pltpu.SemaphoreType.DMA((COPIES,)),
            pltpu.SemaphoreType.DMA((8,)),
        ]
    )
    return pl.pallas_call(
        kernel,
        out_shape=(
            jax.ShapeDtypeStruct(coarse_fields.shape, F32),
            jax.ShapeDtypeStruct(fine_fields.shape, F32),
        ),
        in_specs=[anywhere] * 4 + [pl.BlockSpec(memory_space=pltpu.SMEM)],
        out_specs=(anywhere, anywhere),
        scratch_shapes=scratch,
        compiler_params=pltpu.CompilerParams(
            collective_id=0, has_side_effects=True, vmem_limit_bytes=63 * 1024 * 1024
        ),
        name="two_level_step",
    )(coarse_fields, coarse_wind, fine_fields, fine_wind, fine_owner.reshape((1,)))


def solution(mesh):
    spec = P(None, "gx", "gy", "gz")
    return jax.shard_map(
        shards,
        mesh=mesh,
        in_specs=(spec, spec, spec, spec, P("gx", "gy", "gz")),
        out_specs=(spec, spec),
        check_vma=False,
    )
```

time: 86.9 us -> 69.9 us (0.80)
  Pallas kernels: 77.9 us -> 64.3 us
  local copies, waits for them, and re-layouts: 6.15 us -> 2.93 us
    pallas_call x1, Pallas kernels: 77.9 us -> 64.3 us  [shards(): pl.pallas_call(kernel, out_shape=(jax.ShapeDtypeStruct(coarse_fields.shap...]
    unnamed x10 -> x4, local copies, waits for them, and re-layouts: 6.15 us -> 2.93 us
where the time goes in v2:
time: 69.9 us; the launch traced here: 68.6 us
  Pallas kernels  64.3 us (92%)
  local copies, waits for them, and re-layouts  2.93 us (4%)
  between operations  1.29 us (2%)
    pallas_call x1, Pallas kernels, shards(): pl.pallas_call(kernel, out_shape=(jax.ShapeDtypeStruct(coarse_fields.shap...  64.3 us
    unnamed x4, local copies, waits for them, and re-layouts  2.93 us

profile of v2, /device:TPU:24, one launch (start us, length us, event | category | flops | bytes accessed | tf_op | source)
XLA Modules:
  0.0 68.6 jit_solution(1445541129831365732)
XLA Ops:
  1.3 64.3 %two_level_step.1 = (f32[4,16,16,128]{3,2,1,0:T(8,128)}, f32[4,32,16,128]{3,2,1,0:T(8,128)}) custom-call(f32[4,16,16,128]{3,2,1,0:T(8,128)} %cf.1, f32[3,16,16,128]{3,2,1,0:T(8,128)} %cw.1, f32[4,32,16,128]{3,2,1,0:T(8,128)} %ff.1, f32[3,32,16,128]{3,2,1,0:T(8,128)} %fw.1, s32[1]{0:T(128)} %bitcast.1.own), custom_call_target="tpu_custom_call" | custom-call | tf_op jit(solution)/shard_map/two_level_step/pallas_call | solution.py:506
  65.6 0.0 copy-start
  65.6 2.0 %copy.10 = f32[4,16,16,128]{3,2,1,0:T(8,128)} copy(f32[4,16,16,128]{3,2,1,0:T(8,128)} %get-tuple-element.4) | data formatting | bytes 1048576
  67.6 0.0 copy-done
  67.6 1.0 %copy.11 = f32[4,32,16,128]{3,2,1,0:T(8,128)} copy(f32[4,32,16,128]{3,2,1,0:T(8,128)S(1)} %copy-done) | data formatting | bytes 2097152
Async XLA Ops:
  65.6 2.0 %copy-start = (f32[4,32,16,128]{3,2,1,0:T(8,128)S(1)}, f32[4,32,16,128]{3,2,1,0:T(8,128)}, u32[]{:S(2)}) copy-start(f32[4,32,16,128]{3,2,1,0:T(8,128)} %get-tuple-element.5) | copy-start | bytes 3145732

commit v3 on v2

--- a/solution.py
+++ b/solution.py
@@ -17,10 +17,15 @@
 BOXES = RING_X * RING_Z
 FIELDS, CX, FX, NY, LANES = 4, 16, 32, 16, 128
 LOW, TOP = 8, 24
-PAY = 104
-CHUNKS = 4
-CHUNK_ROWS = 256 // CHUNKS
+PAY = (88, 112, 96)
+OUTER = (2, 1, 1)
+INNER = ((1, 9), (1, 8), (2, 7))
+COLUMNS = (64, 88, 72)
+ENDS = (80, 76, 80)
+RIM = ((0, 72, 112, 80), (9, 80, 48, 84))
+CHUNKS = tuple(tuple(range(4 * c, 4 * c + 4)) for c in range(4))
 COPIES = 72
+VMEM_LIMIT = 62 * 1024 * 1024
 STRIDES = (1, 3)
 
 
@@ -86,9 +91,9 @@
 
 
 def kernel(
-    cf, cw, ff, fw, own, co, fo,
-    tc0, tc1, tc2, uc1, uc2, sc3, wc, sf0, sf1, sf2, sf3, wf,
-    ysend, yrecv, zsend, zrecv, payxs, payzs, slab, corner, face, zt, zface,
+    cf, cw, ff, fw, own, sc3, sf3,
+    tc0, tc1, tc2, uc1, uc2, wc, sf0, sf1, sf2, wf,
+    ysend, yrecv, zsend, zrecv, payxs, payzs, finals, slab, corner, face, zt, zface,
     pairs, avgxs, avgzs, result, w_face, w_avg, w_mix,
     send_sem, recv_sem, load_sem,
 ):
@@ -161,7 +166,7 @@
     there = parts_of(shift)
     home = parts_of((BOXES - shift) % BOXES)
 
-    def start_halos():
+    def start_halos(coarse):
         def both(name, src, dst, first, last, width, end, where):
             halo[name] = (
                 ship(src.at[:, pl.ds(last, width)], where(dst, 0, width), along_row(1)),
@@ -170,10 +175,12 @@
 
         padded = lambda ref, at, width: ref.at[:, pl.ds(at, width), rows, :]
         plain = lambda ref, at, width: ref.at[:, pl.ds(at, width)]
-        both("cf", cf, tc0, 0, CX - 3, 3, CX + 3, padded)
-        both("cw", cw, wc, 0, CX - 2, 2, CX + 2, plain)
-        both("ff", ff, sf0, 0, FX - 3, 3, FX + 3, padded)
-        both("fw", fw, wf, 0, FX - 2, 2, FX + 2, plain)
+        if coarse:
+            both("cf", cf, tc0, 0, CX - 3, 3, CX + 3, padded)
+            both("cw", cw, wc, 0, CX - 2, 2, CX + 2, plain)
+        else:
+            both("ff", ff, sf0, 0, FX - 3, 3, FX + 3, padded)
+            both("fw", fw, wf, 0, FX - 2, 2, FX + 2, plain)
 
     slabs = [tc0, tc1, tc2]
 
@@ -194,16 +201,16 @@
         zero = jnp.zeros((NY, LANES), F32)
         return zero, zero, jnp.zeros((8, LANES), F32)
 
-    def pack_group(k, g, carry):
+    def pack_group(k, g, store, lanes_at, ends_at, carry):
         s = slabs[k]
         low_z, high_z, ends = carry
         lows, highs = [], []
         for h in range(2):
-            at = 2 * g + h + 1
+            at = 2 * g + h + 3 - OUTER[k]
             lows.append(0.75 * s[:, at, LOW + 3, :] + 0.25 * s[:, at, LOW + 4, :])
             highs.append(0.25 * s[:, at, LOW + 11, :] + 0.75 * s[:, at, LOW + 12, :])
             for f in range(FIELDS):
-                p = 8 * g + 4 * h + f
+                p = 8 * g + 4 * h + f + lanes_at
                 q = s[f, at, rows, :]
                 after = pltpu.roll(q, 127, 1)
                 t = jnp.where(lane < 64, 0.75 * q + 0.25 * after, 0.25 * q + 0.75 * after)
@@ -211,38 +218,73 @@
                 high_z = jnp.where(lane == p, pltpu.roll(t, (p - 95 + 128) % 128, 1), high_z)
         low = jnp.concatenate(lows, axis=0)
         high = jnp.concatenate(highs, axis=0)
-        row = pl.multiple_of(8 * g, 8)
-        payxs[k][0, pl.ds(row, 8), :] = jnp.where(
-            lane8 < 64, pltpu.roll(low, 96, 1), pltpu.roll(high, 32, 1)
-        )
+        store(jnp.where(lane8 < 64, pltpu.roll(low, 96, 1), pltpu.roll(high, 32, 1)))
         for n, (value, source) in enumerate(((low, 31), (low, 96), (high, 31), (high, 96))):
-            to = 80 + 4 * g + n
+            to = ends_at + 4 * g + n
             ends = jnp.where(lane8 == to, pltpu.roll(value, (to - source + 128) % 128, 1), ends)
         return low_z, high_z, ends
 
-    def pack_range(k, first, last, carry):
-        return lax.fori_loop(first, last, functools.partial(pack_group, k), carry)
-
-    def pack_end(k, carry):
+    def pack_range(k, begin, end, carry):
+        def group(g, carry):
+            row = pl.multiple_of(8 * g - (8 if k == 0 else 0), 8)
+
+            def store(value):
+                payxs[k][0, pl.ds(row, 8), :] = value
+
+            return pack_group(k, g, store, 0, ENDS[k], carry)
+
+        return lax.fori_loop(begin, end, group, carry)
+
+    def pack_rim():
+        carry = pack_start()
+        for g, row, lanes_at, ends_at in RIM:
+
+            def store(value, row=row):
+                payxs[1][0, row : row + 8, :] = value
+
+            carry = pack_group(0, g, store, lanes_at, ends_at - 4 * g, carry)
+        return carry
+
+    def pack_end(k, carry, rim=None):
         low_z, high_z, ends = carry
-        payxs[k][0, 80:88, :] = jnp.where(lane8 >= 80, ends, low_z[3:11, :])
-        payxs[k][0, 88:90, :] = low_z[11:13, :]
-        payxs[k][0, 92:102, :] = high_z[3:13, :]
+        at = COLUMNS[k]
+        more = jnp.zeros((8, LANES), F32)
+        if rim is not None:
+            low_z, high_z, more = low_z + rim[0], high_z + rim[1], rim[2]
+        payxs[k][0, at : at + 8, :] = low_z[3:11, :] + ends
+        payxs[k][0, at + 8 : at + 10, :] = low_z[11:13, :]
+        payxs[k][0, at + 12 : at + 20, :] = high_z[3:11, :] + more
+        payxs[k][0, at + 20 : at + 22, :] = high_z[11:13, :]
+        shift_x(("pay", k), payxs[k])
 
     def shift_x(name, bufs):
         halo[name, 0] = tuple(
             ship(bufs.at[0], bufs.at[slot], along_x(-slot)) for slot in (1, 2, 3)
         )
 
-    def faces(k):
-        wait((("pay", k), 2))
-        slab[...] = payzs[k][1][there[2]]
-        cols = slab[80:88, :]
-        for g in range(10):
-            corner[8 * g : 8 * g + 8, :] = pltpu.roll(cols, (48 - 4 * g + 128) % 128, 1)
+    def arrive(m):
+        wait((("pay", m), 2))
+        finals[m][...] = payzs[m][1][there[2]]
+
+    def faces(k, late):
+        skip = 8 - 4 * OUTER[k]
+        message, first = finals[k], COLUMNS[k]
+        cells = message[first : first + 8, :]
+        if late:
+            other = finals[1][COLUMNS[1] + 12 : COLUMNS[1] + 20, :]
+            picks = [(g, finals[1], row, other, at) for g, row, _, at in RIM]
+        else:
+            begin, end = (1, 9) if k == 0 else (0, 9)
+            picks = [
+                (g, message, 8 * (g - begin), cells, ENDS[k] + 4 * g) for g in range(begin, end)
+            ]
+        for g, source, row, ends, ends_at in picks:
+            at = 8 * g + skip
+            slab[k, at : at + 8, :] = source[row : row + 8, :]
+            corner[k, at : at + 8, :] = pltpu.roll(ends, (128 - ends_at) % 128, 1)
         parts = []
         for ref in (slab, corner):
-            before, here, after = ref[0:72, :], ref[4:76, :], ref[8:80, :]
+            before, here, after = ref[k, 0:72, :], ref[k, 4:76, :], ref[k, 8:80, :]
             even = 0.25 * before + 0.75 * here
             odd = 0.75 * here + 0.25 * after
             parts.append(jnp.concatenate((even, odd), axis=0))
@@ -261,8 +303,18 @@
 
         lax.fori_loop(0, 9, place, 0)
 
-        for side, first in enumerate((80, 92)):
-            v = slab[first : first + 10, :]
+        for side in range(2):
+            at = first + 12 * side
+            v = message[at : at + 10, :]
+            if late:
+                at = COLUMNS[1] + 12 * side
+                rim = finals[1][at : at + 10, :]
+                lane10 = lax.broadcasted_iota(jnp.int32, (10, LANES), 1)
+                for g, _, lanes_at, _ in RIM:
+                    mine = (lane10 >= 8 * g) & (lane10 < 8 * g + 8)
+                    v = jnp.where(mine, pltpu.roll(rim, (128 - lanes_at) % 128, 1), v)
+            if skip:
+                v = pltpu.roll(v, skip, 1)
             even = 0.25 * pltpu.roll(v, 4, 1) + 0.75 * v
             odd = 0.75 * v + 0.25 * pltpu.roll(v, 124, 1)
             for o, w in enumerate((even, odd)):
@@ -272,7 +324,7 @@
         both = jnp.concatenate(
             [jnp.concatenate((zt[o, 0], zt[o, 1]), axis=1) for o in range(2)], axis=0
         )
-        zface[...] = split_dot(both, w_mix[...]).reshape(2, NY, 256)
+        zface[k] = split_dot(both, w_mix[...]).reshape(2, NY, 256)
 
     def send_edges(k):
         s, off = ((tc0, 3), (uc1, 1), (uc2, 1))[k]
@@ -336,7 +388,7 @@
     def fine_plane(k, x, o, half, first):
         fraction = section_weights[k]
         coefs = [coefficients(wf[d, x + 2], fraction) for d in range(3)]
-        column = zface[o, :, 128 * half : 128 * half + 128]
+        column = zface[k, o, :, 128 * half : 128 * half + 128]
         made = []
         for f in range(FIELDS):
             ghost = pltpu.roll(column, (127 - first - 2 * f + 128) % 128, 1)
@@ -349,52 +401,54 @@
                 fine[k + 1][f, x + 3, rows, :] = new
         return made
 
-    def fine_section(k):
-        def pair(j, carry):
-            fine_plane(k, 2 * j, 0, 0, 8 * j)
-            fine_plane(k, 2 * j + 1, 1, 0, 8 * j)
+    def pair(k, j):
+        return fine_plane(k, 2 * j, 0, 0, 8 * j), fine_plane(k, 2 * j + 1, 1, 0, 8 * j)
+
+    def fine_pairs(k, first, last):
+        def step(j, carry):
+            pair(k, j)
             return carry
 
-        lax.fori_loop(0, 16, pair, 0)
+        lax.fori_loop(first, last, step, 0)
+
+    def fine_rim(k):
         fine_plane(k, -1, 1, 1, 0)
         fine_plane(k, FX, 0, 1, 8)
         if k == 0:
             fine_plane(k, -2, 0, 1, 0)
             fine_plane(k, FX + 1, 1, 1, 8)
 
-    per = 16 // CHUNKS
-
-    def last_section():
-        def pair(j, carry):
-            first = fine_plane(2, 2 * j, 0, 0, 8 * j)
-            second = fine_plane(2, 2 * j + 1, 1, 0, 8 * j)
+    def last_section(c):
+        js = CHUNKS[c]
+
+        def step(j, carry):
+            first, second = pair(2, j)
             for f in range(FIELDS):
                 pairs[j, f] = first[f] + second[f]
             return carry
 
-        for c in range(CHUNKS):
-            lax.fori_loop(c * per, (c + 1) * per, pair, 0)
-            blocks = []
-            for j in range(c * per, (c + 1) * per):
-                for fp in range(2):
-                    halves = [
-                        pairs[j, 2 * fp + n, pl.ds(0, 8, stride=2), :]
-                        + pairs[j, 2 * fp + n, pl.ds(1, 8, stride=2), :]
-                        for n in range(2)
-                    ]
-                    blocks.append(jnp.concatenate(halves, axis=1))
-            avgxs[c][0] = split_dot(jnp.concatenate(blocks, axis=0), w_avg[...])
-            shift_x(("avg", c), avgxs[c])
+        lax.fori_loop(js[0], js[-1] + 1, step, 0)
+        blocks = []
+        for j in js:
+            for fp in range(2):
+                halves = [
+                    pairs[j, 2 * fp + n, pl.ds(0, 8, stride=2), :]
+                    + pairs[j, 2 * fp + n, pl.ds(1, 8, stride=2), :]
+                    for n in range(2)
+                ]
+                blocks.append(jnp.concatenate(halves, axis=1))
+        avgxs[c][0] = split_dot(jnp.concatenate(blocks, axis=0), w_avg[...])
+        shift_x(("avg", c), avgxs[c])
 
     inside = (lane8 >= 32) & (lane8 < 96)
 
     def merge(c):
         wait((("avg", c), 2))
-        result[...] = avgzs[c][1][home[2]].reshape(CHUNK_ROWS // 8, 8, LANES)
-        for j in range(per):
-            x = c * per + j
+        js = CHUNKS[c]
+        result[0 : 16 * len(js), :] = avgzs[c][1][home[2]]
+        for at, x in enumerate(js):
             for fp in range(2):
-                block = result[2 * j + fp]
+                block = result[16 * at + 8 * fp : 16 * at + 8 * fp + 8, :]
                 for n in range(2):
                     f = 2 * fp + n
                     moved = pltpu.roll(block, 32 if n == 0 else 96, 1)
@@ -418,64 +472,69 @@
         )
 
     pl.semaphore_wait(barrier, len(partners))
-    start_halos()
+    start_halos(True)
     in_cf.wait()
-    send_edges(0)
+    pack_end(0, pack_range(0, *INNER[0], pack_start()))
     in_cw.wait()
     slab_range(0, 1, CX - 1)
     slab_range(1, 2, CX - 2)
-    packs = [pack_range(0, 1, 9, pack_start())]
-    packs += [pack_range(k, 2, 8, pack_start()) for k in (1, 2)]
-    for at in (1, CX + 4):
-        tc2[:, at, rows, :] = jnp.zeros((FIELDS, NY, LANES), F32)
+    pack1 = pack_range(1, *INNER[1], pack_start())
+    pack2 = pack_range(2, *INNER[2], pack_start())
     wait("cf")
-    packs[0] = pack_range(0, 0, 1, packs[0])
-    pack_end(0, pack_range(0, 9, 10, packs[0]))
-    shift_x(("pay", 0), payxs[0])
+    rim = pack_rim()
     wait("cw")
     slab_range(0, -2, 1)
     slab_range(0, CX - 1, CX + 2)
-    packs[1] = pack_range(1, 0, 2, packs[1])
-    pack_end(1, pack_range(1, 8, 10, packs[1]))
-    shift_x(("pay", 1), payxs[1])
+    pack1 = pack_range(1, 0, 1, pack1)
+    pack_end(1, pack_range(1, 8, 9, pack1), rim)
+    pay_z(0, 0)
     slab_range(1, -1, 2)
     slab_range(1, CX - 2, CX + 1)
-    packs[2] = pack_range(2, 0, 2, packs[2])
-    pack_end(2, pack_range(2, 8, 10, packs[2]))
-    shift_x(("pay", 2), payxs[2])
+    pack2 = pack_range(2, 0, 2, pack2)
+    pack_end(2, pack_range(2, 7, 9, pack2))
+    send_edges(0)
+    pay_z(0, 1)
     w_face[...] = refine_weights()
     w_avg[...] = average_weights()
     w_mix[...] = interleave_weights()
+    pay_z(1, 0)
+    pay_z(2, 0)
     coarse_section(0)
     send_edges(1)
-    for k in range(3):
-        pay_z(k, 0)
-    pay_z(0, 1)
+    pay_z(1, 1)
+    pay_z(2, 1)
+    start_halos(False)
+    in_ff.wait()
+    in_fw.wait()
+    arrive(0)
+    faces(0, False)
+    fine_pairs(0, 1, 15)
+    arrive(1)
+    faces(1, False)
+    fine_pairs(1, 2, 14)
+    faces(0, True)
+    wait("ff", "fw")
+    pair(0, jnp.int32(0))
+    pair(0, jnp.int32(15))
+    fine_rim(0)
+    fine_pairs(1, 0, 2)
+    fine_pairs(1, 14, 16)
+    fine_rim(1)
+    arrive(2)
+    faces(2, False)
+    for c in range(4):
+        last_section(c)
+    for c in range(4):
+        avg_z(c, 0)
     coarse_section(1)
     send_edges(2)
-    for k in (1, 2):
-        pay_z(k, 1)
-    in_ff.wait()
-    in_fw.wait()
-    wait("ff", "fw")
-    faces(0)
-    fine_section(0)
-    faces(1)
-    fine_section(1)
-    faces(2)
-    last_section()
-    out_fine = load(sf3, fo)
+    for c in range(4):
+        avg_z(c, 1)
     coarse_section(2)
-    for turn in range(2):
-        for c in range(CHUNKS):
-            avg_z(c, turn)
-    for c in range(CHUNKS):
+    for c in range(4):
         merge(c)
-    out_coarse = load(sc3, co)
     for copy in sent:
         copy.wait_send()
-    out_fine.wait()
-    out_coarse.wait()
 
 
 def shards(coarse_fields, coarse_wind, fine_fields, fine_wind, fine_owner):
@@ -484,39 +543,60 @@
     scratch = (
         [vmem(FIELDS, CX + 6, 32, LANES)] * 3
         + [vmem(FIELDS, CX + 2, 32, LANES)] * 2
-        + [vmem(FIELDS, CX, NY, LANES), vmem(3, CX + 4, NY, LANES)]
+        + [vmem(3, CX + 4, NY, LANES)]
         + [vmem(FIELDS, FX + 6, 32, LANES)] * 3
-        + [vmem(FIELDS, FX, NY, LANES), vmem(3, FX + 4, NY, LANES)]
+        + [vmem(3, FX + 4, NY, LANES)]
         + [
             vmem(3, 2, 8, 8, LANES), vmem(3, 2, 8, 8, LANES),
             vmem(3, NY, LANES), vmem(3, NY, LANES),
-            [vmem(RING_X, PAY, LANES)] * 3, [[vmem(3, PAY, LANES)] * 2] * 3,
-            vmem(PAY, LANES), vmem(80, LANES), vmem(18, 8, 256),
-            vmem(2, 2, NY, LANES), vmem(2, NY, 256),
+            [vmem(RING_X, n, LANES) for n in PAY], [[vmem(3, n, LANES)] * 2 for n in PAY],
+            [vmem(n, LANES) for n in PAY], vmem(3, 80, LANES), vmem(3, 80, LANES), vmem(18, 8, 256),
+            vmem(2, 2, NY, LANES), vmem(3, 2, NY, 256),
             vmem(CX, FIELDS, NY, LANES),
-            [vmem(RING_X, CHUNK_ROWS, LANES)] * CHUNKS,
-            [[vmem(3, CHUNK_ROWS, LANES)] * 2] * CHUNKS,
-            vmem(CHUNK_ROWS // 8, 8, LANES),
+            [vmem(RING_X, 16 * len(js), LANES) for js in CHUNKS],
+            [[vmem(3, 16 * len(js), LANES)] * 2 for js in CHUNKS],
+            vmem(16 * len(CHUNKS[0]), LANES),
             pltpu.VMEM((256, 256), BF16), pltpu.VMEM((256, 128), BF16),
             pltpu.VMEM((256, 256), BF16),
             pltpu.SemaphoreType.DMA((COPIES,)), pltpu.SemaphoreType.DMA((COPIES,)),
             pltpu.SemaphoreType.DMA((8,)),
         ]
     )
+    results = pl.pallas_call(
+        kernel,
+        out_shape=(
+            pltpu.VMEM(coarse_fields.shape, F32),
+            pltpu.VMEM(fine_fields.shape, F32),
+        ),
+        in_specs=[anywhere] * 4 + [pl.BlockSpec(memory_space=pltpu.SMEM)],
+        out_specs=(pl.BlockSpec(memory_space=pltpu.VMEM),) * 2,
+        scratch_shapes=scratch,
+        compiler_params=pltpu.CompilerParams(
+            collective_id=0, has_side_effects=True, vmem_limit_bytes=VMEM_LIMIT
+        ),
+        name="two_level_step",
+    )(coarse_fields, coarse_wind, fine_fields, fine_wind, fine_owner.reshape((1,)))
     return pl.pallas_call(
-        kernel,
+        write_out,
         out_shape=(
             jax.ShapeDtypeStruct(coarse_fields.shape, F32),
             jax.ShapeDtypeStruct(fine_fields.shape, F32),
         ),
-        in_specs=[anywhere] * 4 + [pl.BlockSpec(memory_space=pltpu.SMEM)],
+        in_specs=[pl.BlockSpec(memory_space=pl.ANY)] * 2,
         out_specs=(anywhere, anywhere),
-        scratch_shapes=scratch,
-        compiler_params=pltpu.CompilerParams(
-            collective_id=0, has_side_effects=True, vmem_limit_bytes=63 * 1024 * 1024
-        ),
-        name="two_level_step",
-    )(coarse_fields, coarse_wind, fine_fields, fine_wind, fine_owner.reshape((1,)))
+        scratch_shapes=[pltpu.SemaphoreType.DMA((2,))],
+        compiler_params=pltpu.CompilerParams(vmem_limit_bytes=1024 * 1024),
+        name="write_out",
+    )(*results)
+
+
+def write_out(coarse, fine, coarse_out, fine_out, sem):
+    first = pltpu.make_async_copy(fine, fine_out, sem.at[0])
+    second = pltpu.make_async_copy(coarse, coarse_out, sem.at[1])
+    first.start()
+    second.start()
+    first.wait()
+    second.wait()
 
 
 def solution(mesh):

time: 69.9 us -> 67.4 us (0.964); the launches traced: 68.6 us -> 67.3 us
  local copies, waits for them, and re-layouts: 2.93 us -> 0 us
  Pallas kernels: 64.3 us -> 66 us
    unnamed x4 -> x0, local copies, waits for them, and re-layouts: 2.93 us -> none
    pallas_call x1 -> x2, Pallas kernels: 64.3 us -> 66 us  [the longest x1 64.9 us: shards(): pl.pallas_call(kernel, out_shape=(pltpu.VMEM(coarse_fields.shape, F32), p...]
where the time goes in v3:
time: 67.4 us; the launch traced here: 67.3 us
  Pallas kernels  66 us (98%)
  between operations  1.29 us (2%)
    pallas_call x1, Pallas kernels, shards(): pl.pallas_call(kernel, out_shape=(pltpu.VMEM(coarse_fields.shape, F32), p...  64.9 us

profile of v3, /device:TPU:24, one launch (start us, length us, event | category | flops | bytes accessed | tf_op | source)
XLA Modules:
  0.0 67.3 jit_solution(12684964549051779325)
XLA Ops:
  1.3 64.9 %two_level_step.1 = (f32[4,16,16,128]{3,2,1,0:T(8,128)S(1)}, f32[4,32,16,128]{3,2,1,0:T(8,128)S(1)}) custom-call(f32[4,16,16,128]{3,2,1,0:T(8,128)} %cf.1, f32[3,16,16,128]{3,2,1,0:T(8,128)} %cw.1, f32[4,32,16,128]{3,2,1,0:T(8,128)} %ff.1, f32[3,32,16,128]{3,2,1,0:T(8,128)} %fw.1, s32[1]{0:T(128)} %bitcast.1.own), custom_call_target="tpu_custom_call" | custom-call | tf_op jit(solution)/shard_map/two_level_step/pallas_call | solution.py:565
  66.2 1.2 %write_out.1 = (f32[4,16,16,128]{3,2,1,0:T(8,128)}, f32[4,32,16,128]{3,2,1,0:T(8,128)}) custom-call(f32[4,16,16,128]{3,2,1,0:T(8,128)S(1)} %get-tuple-element.4.coarse, f32[4,32,16,128]{3,2,1,0:T(8,128)S(1)} %get-tuple-element.5.fine), custom_call_target="tpu_custom_call" | custom-call | tf_op jit(solution)/shard_map/write_out/pallas_call | solution.py:579

commit v4 on v3

--- a/solution.py
+++ b/solution.py
@@ -499,11 +499,11 @@
     w_mix[...] = interleave_weights()
     pay_z(1, 0)
     pay_z(2, 0)
+    start_halos(False)
     coarse_section(0)
     send_edges(1)
     pay_z(1, 1)
     pay_z(2, 1)
-    start_halos(False)
     in_ff.wait()
     in_fw.wait()
     arrive(0)

time: 67.4 us -> 67 us (level)
  Pallas kernels: 66 us -> 65.2 us
    pallas_call x1, Pallas kernels: 64.9 us -> 64 us  [shards(): pl.pallas_call(kernel, out_shape=(pltpu.VMEM(coarse_fields.shape, F32), p...]
where the time goes in v4:
time: 67 us; the launch traced here: 66.4 us
  Pallas kernels  65.2 us (97%)
  between operations  1.29 us (2%)
    pallas_call x1, Pallas kernels, shards(): pl.pallas_call(kernel, out_shape=(pltpu.VMEM(coarse_fields.shape, F32), p...  64 us

profile of v4, /device:TPU:24, one launch (start us, length us, event | category | flops | bytes accessed | tf_op | source)
XLA Modules:
  0.0 66.4 jit_solution(14110846627883858086)
XLA Ops:
  1.3 64.0 %two_level_step.1 = (f32[4,16,16,128]{3,2,1,0:T(8,128)S(1)}, f32[4,32,16,128]{3,2,1,0:T(8,128)S(1)}) custom-call(f32[4,16,16,128]{3,2,1,0:T(8,128)} %cf.1, f32[3,16,16,128]{3,2,1,0:T(8,128)} %cw.1, f32[4,32,16,128]{3,2,1,0:T(8,128)} %ff.1, f32[3,32,16,128]{3,2,1,0:T(8,128)} %fw.1, s32[1]{0:T(128)} %bitcast.1.own), custom_call_target="tpu_custom_call" | custom-call | tf_op jit(solution)/shard_map/two_level_step/pallas_call | solution.py:565
  65.3 1.2 %write_out.1 = (f32[4,16,16,128]{3,2,1,0:T(8,128)}, f32[4,32,16,128]{3,2,1,0:T(8,128)}) custom-call(f32[4,16,16,128]{3,2,1,0:T(8,128)S(1)} %get-tuple-element.4.coarse, f32[4,32,16,128]{3,2,1,0:T(8,128)S(1)} %get-tuple-element.5.fine), custom_call_target="tpu_custom_call" | custom-call | tf_op jit(solution)/shard_map/write_out/pallas_call | solution.py:579
